TPU v7x, 512 devices: a whole 4x4x16 slice. The times are simulated.
512 devices in a mesh: grp: 16 (over z), dev: 32 (over y, x, core).
Axes of the slice: x: 4, y: 4, z: 16, core: 2. Of those that a mesh axis runs over, the one named last changes fastest.
Arguments:
- positions: float32 [3, 524288], P(None, ('grp', 'dev')), may hold values from -1 to 1
- forces: float32 [3, 524288], P(None, ('grp', 'dev')), may hold values from -4 to 4
- volumes: float32 [524288], P(('grp', 'dev')), may hold values from 0.02 to 0.2
- dest_bin: int32 [524288, 1], P(('grp', 'dev')), may hold values from 0 to 511; in each aligned block of 1024 rows (0 to 1023, 1024 to 2047, ...) at most 4 rows name the same one
- element: int32 [524288], P(('grp', 'dev')), may hold values from 0 to 127
Outputs:
- assembled: float32 [4, 216, 65536], P(None, None, ('grp', 'dev'))
Inputs may be any that keep to these rules, and one draw needn't show every extreme that they name: `dest_bin`: no more than 4 of the particles of one device share a bin, and that number is reached.
All inputs are finite; a program needn't handle non-finite values.
Results may differ from a plain program's by a relative error of at most 0.0028.
Values sent between devices are 32-bit elements; how exact they have to be, the bound alone decides.
A program may use at most 64 MiB of HBM per device.

v0:
```python
import math

import jax
import jax.numpy as jnp
from jax import lax
from jax.sharding import PartitionSpec as P

E_DEV = 128


gll_points = (
    -1.0,
    -0.765055323929465,
    -0.285231516480645,
    0.285231516480645,
    0.765055323929465,
    1.0,
)


def extended_2(block, sides, width):
    for axis, dim in sides:
        count = lax.axis_size(axis)
        forward = [(i, i + 1) for i in range(count - 1)]
        backward = [(target, source) for source, target in forward]
        low = lax.ppermute(
            lax.slice_in_dim(block, block.shape[dim] - width, None, axis=dim), axis, forward
        )
        high = lax.ppermute(lax.slice_in_dim(block, 0, width, axis=dim), axis, backward)
        block = jnp.concatenate([low, block, high], axis=dim)
    return block


def tensor_weights(coords):
    nodes = jnp.array(gll_points, jnp.float32)
    w_r = jnp.exp(-((nodes[:, None] - coords[0][None, :]) ** 2) / 0.5)
    w_s = jnp.exp(-((nodes[:, None] - coords[1][None, :]) ** 2) / 0.5)
    w_t = jnp.exp(-((nodes[:, None] - coords[2][None, :]) ** 2) / 0.5)
    full = w_r[:, None, None, :] * w_s[None, :, None, :] * w_t[None, None, :, :]
    return full.reshape(216, coords.shape[1])


def per_device(positions, forces, volumes, dest_bin, element):
    n_grp = lax.axis_size("grp")
    n_dev = lax.axis_size("dev")
    bins = n_grp * n_dev
    count = dest_bin.shape[0]
    slots_per = max(2, 2 * count // bins)
    target = dest_bin[:, 0]
    order = jnp.argsort(target, stable=True)
    sorted_bin = target[order]
    tally = jax.ops.segment_sum(jnp.ones((count,), jnp.int32), target, num_segments=bins)
    starts = jnp.cumsum(tally) - tally
    rank = jnp.arange(count, dtype=jnp.int32) - starts[sorted_bin]
    slot = sorted_bin * slots_per + rank
    feats = jnp.concatenate([positions, forces, volumes[None, :]], 0)
    width = bins * slots_per
    packed = jnp.zeros((7, width), jnp.float32).at[:, slot].set(feats[:, order])
    labels = jnp.zeros((1, width), jnp.int32).at[:, slot].set(element[order][None, :])
    packed = packed.reshape(7, n_grp, n_dev, slots_per)
    labels = labels.reshape(1, n_grp, n_dev, slots_per)
    moved = (
        lax.all_to_all(
            lax.all_to_all(packed, "grp", split_axis=1, concat_axis=1, tiled=True),
            "dev",
            split_axis=2,
            concat_axis=2,
            tiled=True,
        ),
        lax.all_to_all(
            lax.all_to_all(labels, "grp", split_axis=1, concat_axis=1, tiled=True),
            "dev",
            split_axis=2,
            concat_axis=2,
            tiled=True,
        ),
    )
    rows = moved[0].reshape(7, width)
    ids = moved[1].reshape(width)
    block = math.gcd(width, 2048)
    nblk = width // block
    rows_b = rows.reshape(7, nblk, block).transpose(1, 0, 2)
    ids_b = ids.reshape(nblk, block)
    columns = jnp.arange(E_DEV, dtype=jnp.int32)

    def step(acc, item):
        part, idx = item
        weights = tensor_weights(part[0:3])
        values = jnp.concatenate([part[6:7], part[3:6]], 0)
        contrib = (values[:, None, :] * weights[None]).reshape(864, block).astype(jnp.bfloat16)
        onehot = (idx[:, None] == columns[None, :]).astype(jnp.bfloat16)
        return (acc + jnp.dot(contrib, onehot, preferred_element_type=jnp.float32), None)

    acc, _ = lax.scan(step, jnp.zeros((864, E_DEV), jnp.float32), (rows_b, ids_b))
    raw = acc.reshape(4, 6, 6, 6, E_DEV)
    raw0 = raw[:, :, :, 0, :]
    raw5 = raw[:, :, :, 5, :]
    rim = jnp.stack([raw0[..., 0], raw5[..., -1]], -1).reshape(144, 2)
    extended = extended_2(rim, ((("grp", "dev"), 1),), 1)
    prev_five = extended[:, 0].reshape(4, 6, 6)
    next_zero = extended[:, 3].reshape(4, 6, 6)
    after = jnp.concatenate([raw0[..., 1:], next_zero[..., None]], -1)
    before = jnp.concatenate([prev_five[..., None], raw5[..., :-1]], -1)
    out = raw.at[:, :, :, 5, :].add(after)
    out = out.at[:, :, :, 0, :].add(before)
    return out.reshape(4, 216, E_DEV)


def solution(mesh):
    in_specs = (
        P(None, ("grp", "dev")),
        P(None, ("grp", "dev")),
        P(("grp", "dev")),
        P(("grp", "dev"), None),
        P(("grp", "dev")),
    )
    out_specs = P(None, None, ("grp", "dev"))
    return jax.shard_map(
        per_device, mesh=mesh, in_specs=in_specs, out_specs=out_specs, check_vma=False
    )
```

profile of v0, /device:TPU:32, one launch (start us, length us, event | category | flops | bytes accessed | tf_op | source)
XLA Modules:
  0.0 135.4 jit_solution(7228339819571395291)
XLA Ops:
  0.0 7.9 %scatter_custom_fusion = s32[512]{0:T(512)S(1)} fusion(s32[1024]{0:T(1024)} %bitcast.50, s32[1024]{0:T(1024)S(1)} %broadcast.188, s32[]{:T(128)} %constant.83.clone.1), kind=kCustom, calls=%fused_computation.40 | custom fusion | flops 1024 | bytes 2560 | tf_op jit(solution)/shard_map/scatter-add | solution.py:52
  7.9 0.3 reduce-window.9
  8.3 0.1 slice_reduce_fusion
  8.5 5.1 %sort.17 = (s32[1024]{0:T(1024)}, s32[1024]{0:T(1024)S(1)}) sort(s32[1024]{0:T(1024)} %bitcast.51, s32[1024]{0:T(1024)S(1)} %iota.12), dimensions={0}, to_apply=%region_0.0 | sort | flops 10240 | bytes 16384 | tf_op jit(solution)/shard_map/jit(argsort)/sort | solution.py:50
  13.6 4.5 %gather_fusion = s32[1024]{0:T(1024)S(1)} fusion(s32[1024]{0:T(1024)S(1)} %bitcast.52, s32[1024]{0:T(1024)S(1)} %fusion.9), kind=kCustom, calls=%fused_computation | custom fusion | bytes 12288 | tf_op jit(solution)/shard_map/gather | solution.py:51
  18.1 4.5 %gather_fusion.2 = s32[1024]{0:T(1024)S(1)} fusion(s32[1024]{0:T(1024)S(1)} %copy-done, s32[1024]{0:T(1024)S(1)} %fusion.9), kind=kCustom, calls=%fused_computation.3 | custom fusion | bytes 12288 | tf_op jit(solution)/shard_map/gather | solution.py:59
  22.7 6.9 %gather_fusion.1 = s32[1024]{0:T(1024)S(1)} fusion(s32[512]{0:T(512)S(1)} %bitcast_subtract_fusion, s32[1024]{0:T(1024)S(1)} %broadcast_clamp_fusion), kind=kCustom, calls=%fused_computation.1 | custom fusion | bytes 12288 | tf_op jit(solution)/shard_map/gather | solution.py:54
  29.6 4.3 %scatter_custom_fusion.2 = s32[2048]{0:T(1024)S(1)} fusion(s32[1024]{0:T(1024)S(1)} %bitcast.70, s32[1024]{0:T(1024)S(1)} %gather_fusion.2, s32[]{:T(128)} %constant.83.clone.1), kind=kCustom, calls=%fused_computation.35 | custom fusion | bytes 8196 | tf_op jit(solution)/shard_map/scatter | solution.py:59
  33.9 0.3 reshape.287
  34.2 0.2 copy.98
  34.4 0.7 reshape.387
  35.1 15.2 %all-to-all-start.2 = ((s32[16,1,128]{2,1,0:T(1,128)}), s32[16,1,128]{2,1,0:T(1,128)S(1)}, u32[]{:S(2)}, u32[]{:S(2)}) async-start(s32[16,1,128]{2,1,0:T(1,128)} %reshape.387), calls=%async_computation.2 | async-start | bytes 16384 | tf_op jit(solution)/shard_map/all_to_all | solution.py:71
  50.3 0.2 copy.90
  50.6 6.9 %scatter_custom_fusion.1 = f32[7,2048]{0,1:T(8,128)S(1)} fusion(s32[1024]{0:T(1024)S(1)} %bitcast.71, f32[7,1024]{0,1:T(8,128)S(1)} %copy.90, s32[1024]{0:T(1024)S(1)} %fusion.9, f32[]{:T(128)} %constant.82.clone.1), kind=kCustom, calls=%fused_computation.14 | custom fusion | bytes 57348 | tf_op jit(solution)/shard_map/scatter | solution.py:58
  57.5 0.5 copy.91
  57.9 0.8 reshape.383
  58.8 2.7 %all-to-all-done.2 = s32[16,1,128]{2,1,0:T(1,128)S(1)} async-done(((s32[16,1,128]{2,1,0:T(1,128)}), s32[16,1,128]{2,1,0:T(1,128)S(1)}, u32[]{:S(2)}, u32[]{:S(2)}) %all-to-all-start.2) | async-done | bytes 8224 | tf_op jit(solution)/shard_map/all_to_all | solution.py:71
  61.4 9.4 %all-to-all-start = ((f32[16,1,896]{2,1,0:T(1,128)}), f32[16,1,896]{2,1,0:T(1,128)S(1)}, u32[]{:S(2)}, u32[]{:S(2)}) async-start(f32[16,1,896]{2,1,0:T(1,128)} %reshape.383), calls=%async_computation | async-start | bytes 114688 | tf_op jit(solution)/shard_map/all_to_all | solution.py:64
  70.8 0.6 broadcast.225
  71.4 0.7 reduce.16
  72.2 0.7 copy.99
  72.9 9.6 %all-to-all-done = f32[16,1,896]{2,1,0:T(1,128)S(1)} async-done(((f32[16,1,896]{2,1,0:T(1,128)}), f32[16,1,896]{2,1,0:T(1,128)S(1)}, u32[]{:S(2)}, u32[]{:S(2)}) %all-to-all-start) | async-done | bytes 57376 | tf_op jit(solution)/shard_map/all_to_all | solution.py:64
  82.5 7.3 %all-to-all-start.3 = ((s32[1,16,32,4]{1,3,0,2:T(4,128)}), s32[1,16,32,4]{1,3,0,2:T(4,128)S(1)}, u32[]{:S(2)}, u32[]{:S(2)}) async-start(s32[1,16,32,4]{1,3,0,2:T(4,128)} %copy.99), calls=%async_computation.3 | async-start | bytes 131072 | tf_op jit(solution)/shard_map/all_to_all | solution.py:70
  89.8 0.5 broadcast.223
  90.4 0.7 reduce.14
  91.1 0.2 reshape.384
  91.3 0.2 copy.92
  91.6 1.0 reshape.385
  92.6 4.8 %all-to-all-done.3 = s32[1,16,32,4]{1,3,0,2:T(4,128)S(1)} async-done(((s32[1,16,32,4]{1,3,0,2:T(4,128)}), s32[1,16,32,4]{1,3,0,2:T(4,128)S(1)}, u32[]{:S(2)}, u32[]{:S(2)}) %all-to-all-start.3) | async-done | bytes 8224 | tf_op jit(solution)/shard_map/all_to_all | solution.py:70
  97.3 4.0 %all-to-all-start.1 = ((f32[32,1,448]{2,1,0:T(1,128)}), f32[32,1,448]{2,1,0:T(1,128)S(1)}, u32[]{:S(2)}, u32[]{:S(2)}) async-start(f32[32,1,448]{2,1,0:T(1,128)} %reshape.385), calls=%async_computation.1 | async-start | bytes 131072 | tf_op jit(solution)/shard_map/all_to_all | solution.py:63
  101.4 0.4 copy.100
  101.7 0.2 eq.22
  101.9 6.8 %all-to-all-done.1 = f32[32,1,448]{2,1,0:T(1,128)S(1)} async-done(((f32[32,1,448]{2,1,0:T(1,128)}), f32[32,1,448]{2,1,0:T(1,128)S(1)}, u32[]{:S(2)}, u32[]{:S(2)}) %all-to-all-start.1) | async-done | bytes 57376 | tf_op jit(solution)/shard_map/all_to_all | solution.py:63
  108.7 0.8 reduce.15
  109.4 0.3 reshape.386
  109.8 0.4 copy.93
  110.2 0.2 slice.131
  110.3 0.4 copy.97
  110.7 0.2 sub.90
  110.9 0.4 copy.96
  111.2 0.2 sub.87
  111.4 0.4 copy.95
  111.8 0.2 sub.84
  111.9 0.8 copy.94
  112.8 0.5 slice.133
  113.3 0.1 multiply_exponential_fusion.2
  113.5 0.3 broadcast_multiply_fusion
  113.7 2.0 %fusion = f32[4,6,6,6,128]{4,3,2,1,0:T(8,128)S(1)} fusion(f32[6,6,6,2048]{3,2,1,0:T(8,128)S(1)} %broadcast_multiply_fusion, f32[4,2048]{1,0:T(4,128)S(1)} %pad_maximum_fusion.2, s32[2048]{0:T(1024)S(1)} %eq.22), kind=kOutput, calls=%fused_computation.8 | convolution fusion | flops 456785920 | bytes 2252800 | tf_op jit(solution)/shard_map/while/body/eval_jaxpr/dot_general | solution.py:92
  115.7 0.1 fusion.14
  116.1 0.3 copy.103
  116.5 4.0 %collective-permute-start = (f32[144,1]{0,1:T(1,128)S(1)}, f32[144,1]{0,1:T(1,128)S(1)}, u32[]{:S(2)}, u32[]{:S(2)}) collective-permute-start(f32[144,1]{0,1:T(1,128)S(1)} %get-tuple-element.56), channel_id=1, source_target_pairs={{1,0},{2,1},{3,2},{4,3},{5,4},{6,5},{7,6},{8,7},{9,8},{10,9},{11,1... | collective-permute-start | bytes 1736 | tf_op jit(solution)/shard_map/ppermute | solution.py:29
  120.5 1.9 %collective-permute-start.1 = (f32[144,1]{0,1:T(1,128)S(1)}, f32[144,1]{0,1:T(1,128)S(1)}, u32[]{:S(2)}, u32[]{:S(2)}) collective-permute-start(f32[144,1]{0,1:T(1,128)S(1)} %get-tuple-element.55), channel_id=1, source_target_pairs={{0,1},{1,2},{2,3},{3,4},{4,5},{5,6},{6,7},{7,8},{8,9},{9,10},{10,1... | collective-permute-start | bytes 1736 | tf_op jit(solution)/shard_map/ppermute | solution.py:26
  122.6 0.5 broadcast.221
  123.1 0.7 reduce.12
  123.8 5.8 %collective-permute-done.1 = f32[144,1]{0,1:T(1,128)S(1)} collective-permute-done((f32[144,1]{0,1:T(1,128)S(1)}, f32[144,1]{0,1:T(1,128)S(1)}, u32[]{:S(2)}, u32[]{:S(2)}) %collective-permute-start.1) | collective-permute-done | bytes 608 | tf_op jit(solution)/shard_map/ppermute | solution.py:26
  129.6 0.7 reduce.13
  130.4 0.3 copy.106
  130.6 0.3 copy.104
  130.9 0.1 maximum_bitcast_fusion
  131.0 0.1 copy_add_fusion
  131.3 1.5 %scatter-add.18 = f32[4,6,6,6,128]{4,3,2,1,0:T(8,128)S(1)} dynamic-update-slice(f32[4,6,6,6,128]{4,3,2,1,0:T(8,128)S(1)} %fusion, f32[4,6,6,1,128]{4,3,2,1,0:T(1,128)S(1)} %copy_add_fusion, s32[]{:T(128)} %constant.83.clone.1, s32[]{:T(128)} %constant.83.clone.1, s32[]{:T(128)} %constant.83.clone.1, s32[]{:T(128)} %constant.90.clone.1, s32[]{:T(128)} %constant.83.clone.1) | dynamic-update-slice | bytes 147460 | tf_op jit(solution)/shard_map/scatter-add | solution.py:104
  132.9 1.5 %scatter-add.19 = f32[4,6,6,6,128]{4,3,2,1,0:T(8,128)S(1)} dynamic-update-slice(f32[4,6,6,6,128]{4,3,2,1,0:T(8,128)S(1)} %scatter-add.18, f32[4,6,6,1,128]{4,3,2,1,0:T(1,128)S(1)} %slice_add_fusion, s32[]{:T(128)} %constant.83.clone.1, s32[]{:T(128)} %constant.83.clone.1, s32[]{:T(128)} %constant.83.clone.1, s32[]{:T(128)} %constant.83.clone.1, s32[]{:T(128)} %constant.83.clone.1) | dynamic-update-slice | bytes 147460 | tf_op jit(solution)/shard_map/scatter-add | solution.py:105
  134.3 0.3 copy.108
  134.6 0.8 copy.109
  (38 shorter events, 1.3 us)
Async XLA Ops:
  0.0 18.1 %copy-start = (s32[1024]{0:T(1024)S(1)}, s32[1024]{0:T(1024)}, u32[]{:S(2)}) copy-start(s32[1024]{0:T(1024)} %param.14) | copy-start | bytes 12292
  0.0 13.6 %copy-start.1 = (s32[1024,1]{0,1:T(1,128)S(1)}, s32[1024,1]{0,1:T(1,128)}, u32[]{:S(2)}) copy-start(s32[1024,1]{0,1:T(1,128)} %param.13) | copy-start | bytes 12292
  22.7 27.6 %copy-start.2 = (f32[3,1024]{1,0:T(4,128)S(1)}, f32[3,1024]{1,0:T(4,128)}, u32[]{:S(2)}) copy-start(f32[3,1024]{1,0:T(4,128)} %param.11) | copy-start | bytes 36868
  22.7 27.6 %copy-start.3 = (f32[3,1024]{1,0:T(4,128)S(1)}, f32[3,1024]{1,0:T(4,128)}, u32[]{:S(2)}) copy-start(f32[3,1024]{1,0:T(4,128)} %param.10) | copy-start | bytes 36868
  22.7 27.6 %copy-start.4 = (f32[1024]{0:T(1024)S(1)}, f32[1024]{0:T(1024)}, u32[]{:S(2)}) copy-start(f32[1024]{0:T(1024)} %param.12) | copy-start | bytes 12292
  35.1 26.3 %all-to-all-start.2 = ((s32[16,1,128]{2,1,0:T(1,128)}), s32[16,1,128]{2,1,0:T(1,128)S(1)}, u32[]{:S(2)}, u32[]{:S(2)}) async-start(s32[16,1,128]{2,1,0:T(1,128)} %reshape.387), calls=%async_computation.2 | async-start | bytes 16384 | tf_op jit(solution)/shard_map/all_to_all | solution.py:71
  61.4 21.1 %all-to-all-start = ((f32[16,1,896]{2,1,0:T(1,128)}), f32[16,1,896]{2,1,0:T(1,128)S(1)}, u32[]{:S(2)}, u32[]{:S(2)}) async-start(f32[16,1,896]{2,1,0:T(1,128)} %reshape.383), calls=%async_computation | async-start | bytes 114688 | tf_op jit(solution)/shard_map/all_to_all | solution.py:64
  82.5 14.8 %all-to-all-start.3 = ((s32[1,16,32,4]{1,3,0,2:T(4,128)}), s32[1,16,32,4]{1,3,0,2:T(4,128)S(1)}, u32[]{:S(2)}, u32[]{:S(2)}) async-start(s32[1,16,32,4]{1,3,0,2:T(4,128)} %copy.99), calls=%async_computation.3 | async-start | bytes 131072 | tf_op jit(solution)/shard_map/all_to_all | solution.py:70
  97.3 11.3 %all-to-all-start.1 = ((f32[32,1,448]{2,1,0:T(1,128)}), f32[32,1,448]{2,1,0:T(1,128)S(1)}, u32[]{:S(2)}, u32[]{:S(2)}) async-start(f32[32,1,448]{2,1,0:T(1,128)} %reshape.385), calls=%async_computation.1 | async-start | bytes 131072 | tf_op jit(solution)/shard_map/all_to_all | solution.py:63
  109.7 3.5 %copy-start.5 = (f32[6]{0:T(128)S(1)}, f32[6]{0:T(128)}, u32[]{:S(2)}) copy-start(f32[6]{0:T(128)} %constant.91.clone) | copy-start | bytes 76
  116.5 6.0 %collective-permute-start = (f32[144,1]{0,1:T(1,128)S(1)}, f32[144,1]{0,1:T(1,128)S(1)}, u32[]{:S(2)}, u32[]{:S(2)}) collective-permute-start(f32[144,1]{0,1:T(1,128)S(1)} %get-tuple-element.56), channel_id=1, source_target_pairs={{1,0},{2,1},{3,2},{4,3},{5,4},{6,5},{7,6},{8,7},{9,8},{10,9},{11,1... | collective-permute-start | bytes 1736 | tf_op jit(solution)/shard_map/ppermute | solution.py:29
  120.5 9.1 %collective-permute-start.1 = (f32[144,1]{0,1:T(1,128)S(1)}, f32[144,1]{0,1:T(1,128)S(1)}, u32[]{:S(2)}, u32[]{:S(2)}) collective-permute-start(f32[144,1]{0,1:T(1,128)S(1)} %get-tuple-element.55), channel_id=1, source_target_pairs={{0,1},{1,2},{2,3},{3,4},{4,5},{5,6},{6,7},{7,8},{8,9},{9,10},{10,1... | collective-permute-start | bytes 1736 | tf_op jit(solution)/shard_map/ppermute | solution.py:26
where the time goes:
time: 136 us; the launch traced here: 135 us
  local copies, waits for them, and re-layouts  43.6 us (32%)
  starting transfers between devices  41.9 us (31%)
  waiting for transfers between devices  29.6 us (22%)
  other arithmetic  17.9 us (13%)
  matrix products  1.95 us (1%)
    all_to_all x1, starting transfers between devices, per_device(): lax.all_to_all(labels, 'grp', split_axis=1, concat_axis=1, tiled=True)  15.2 us
    all_to_all x1, waiting for transfers between devices, per_device(): lax.all_to_all(packed, 'grp', split_axis=1, concat_axis=1, tiled=True)  9.62 us
    all_to_all x1, starting transfers between devices, per_device(): lax.all_to_all(packed, 'grp', split_axis=1, concat_axis=1, tiled=True)  9.38 us
    scatter-add x1, other arithmetic, per_device(): jax.ops.segment_sum(jnp.ones((count,), jnp.int32), target, num_segments=b...  7.88 us
    all_to_all x1, starting transfers between devices, per_device(): lax.all_to_all(lax.all_to_all(labels, 'grp', split_axis=1, concat_axis=1,...  7.32 us
    scatter x1, local copies, waits for them, and re-layouts, per_device(): packed = jnp.zeros((7, width), jnp.float32).at[:, slot].set(feats[:, order])  6.89 us
    gather x1, local copies, waits for them, and re-layouts, per_device(): rank = jnp.arange(count, dtype=jnp.int32) - starts[sorted_bin]  6.87 us
    all_to_all x1, waiting for transfers between devices, per_device(): lax.all_to_all(lax.all_to_all(packed, 'grp', split_axis=1, concat_axis=1,...  6.77 us
  transfers between devices with their start and end apart: 6, of which 5 were waited for; matrix products, arithmetic and copies ran while one was open for 11% of the time, Pallas kernels for 0%

commit v1 on v0

v1 whole, which is shorter than its diff:
```python
import functools

import jax
import jax.numpy as jnp
from jax import lax
from jax.experimental import pallas as pl
from jax.experimental.pallas import tpu as pltpu
from jax.sharding import PartitionSpec as P

MESH = pl.DeviceIdType.MESH
F32, BF16, I32 = jnp.float32, jnp.bfloat16, jnp.int32

GRP, DEV, SLOTS, LOCAL, ELEMS = 16, 32, 4, 1024, 128
TILE = 128
NEAR = 4

gll_points = (
    -1.0,
    -0.765055323929465,
    -0.285231516480645,
    0.285231516480645,
    0.765055323929465,
    1.0,
)


def iota(shape, axis):
    return lax.broadcasted_iota(I32, shape, axis)


def roll(x, shift, axis):
    shift = shift % x.shape[axis]
    return x if shift == 0 else pltpu.roll(x, shift, axis)


def dot_nt(a, b):
    return lax.dot_general(a, b, (((1,), (1,)), ((), ())), preferred_element_type=F32)


def rank_in_bin(target):
    blocks = LOCAL // TILE
    row = target.astype(F32)
    parts = [row[:, b * TILE:(b + 1) * TILE] for b in range(blocks)]
    columns = [jnp.transpose(jnp.broadcast_to(part, (TILE, TILE))) for part in parts]
    earlier = iota((TILE, TILE), 0) < iota((TILE, TILE), 1)
    ranks = []
    for p in range(blocks):
        own = (columns[p] == parts[p]) & earlier
        total = jnp.where(own, 1.0, 0.0)
        for q in range(p):
            total = total + jnp.where(columns[q] == parts[p], 1.0, 0.0)
        ranks.append(jnp.sum(total, axis=0, keepdims=True))
    return jnp.concatenate(ranks, axis=1).astype(I32)


def pieces(x):
    high = x.astype(BF16).astype(F32)
    rest = x - high
    mid = rest.astype(BF16).astype(F32)
    return high, mid, rest - mid


def pack(positions, forces, volumes, target, element):
    code = (target // DEV) * SLOTS + rank_in_bin(target)
    lane_of = iota((TILE, LOCAL), 0)
    mine = (lane_of // 4) == target % DEV
    sub = iota((8, LOCAL), 0) % 4
    rows = (
        (positions[0:1], positions[1:2], positions[2:3], element.astype(F32)),
        (forces[0:1], forces[1:2], forces[2:3], volumes),
    )
    out = None
    for half, (f0, f1, f2, f3) in enumerate(rows):
        feats = jnp.where(sub == 0, f0, jnp.where(sub == 1, f1, jnp.where(sub == 2, f2, f3)))
        left = jnp.concatenate(
            [
                jnp.where(mine, jnp.concatenate([piece] * 16, axis=0), 0.0).astype(BF16)
                for piece in pieces(feats)
            ],
            axis=0,
        )
        right = jnp.where(lane_of == code + half * 64, 1.0, 0.0).astype(BF16)
        prod = dot_nt(left, right)
        part = prod[0:128] + prod[128:256] + prod[256:384]
        out = part if out is None else out + part
    return out


def to_group_tiles(tiles):
    sub, lane = iota((8, TILE), 0), iota((8, TILE), 1)
    keep = (sub // 4) == (lane // 64)
    tiles = [jnp.where(keep, x, roll(roll(x, 4, 0), 64, 1)) for x in tiles]
    for bit in range(4):
        step = 4 << bit
        low = (lane // step) % 2 == 0
        new = list(tiles)
        for v in range(16):
            if not (v >> bit) & 1:
                a, b = tiles[v], tiles[v | (1 << bit)]
                new[v] = jnp.where(low, a, roll(b, step, 1))
                new[v | (1 << bit)] = jnp.where(low, roll(a, -step, 1), b)
        tiles = new
    return tiles


def by_row(sub, labels, parts):
    out = parts[labels[0]]
    for s in range(1, 8):
        if labels[s] != labels[s - 1]:
            out = jnp.where(sub >= s, parts[labels[s]], out)
    return out


def weigh(x):
    width = x.shape[1]
    shape = (8, width)
    sub = iota(shape, 0)
    nodes = jnp.full(shape, gll_points[5], F32)
    for n in range(5):
        nodes = jnp.where(sub == n, gll_points[n], nodes)
    w_r, w_s, w_t = [jnp.exp(-((nodes - x[d:d + 1]) ** 2) / 0.5) for d in range(3)]
    r_rows = [jnp.broadcast_to(w_r[i:i + 1], shape) for i in range(6)]
    s_cycle = (
        jnp.where(sub < 6, w_s, roll(w_s, 6, 0)),
        jnp.where(sub < 4, roll(w_s, 6, 0), roll(w_s, 4, 0)),
        jnp.where(sub < 2, roll(w_s, 4, 0), roll(w_s, 2, 0)),
    )
    faces = [
        by_row(sub, [((8 * b + s) % 36) // 6 for s in range(8)], r_rows) * s_cycle[b % 3]
        for b in range(9)
    ]
    values = [jnp.broadcast_to(x[d:d + 1], shape) for d in (7, 4, 5, 6)]
    scaled = [
        by_row(sub, [(8 * b + s) // 36 for s in range(8)], values) * faces[b % 9]
        for b in range(18)
    ]
    onehot = jnp.where(iota((ELEMS, width), 0) == x[3:4].astype(I32), 1.0, 0.0).astype(BF16)
    return scaled, w_t, onehot


def slab(scaled, w_t, onehot, k):
    weight = jnp.broadcast_to(w_t[k:k + 1], scaled[0].shape)
    contrib = jnp.concatenate([part * weight for part in scaled], axis=0).astype(BF16)
    return dot_nt(contrib, onehot)


def kernel(
    pos_ref, frc_ref, vol_ref, bin_ref, elem_ref, out_ref,
    send1, recv1, send2, recv2, acc, rim_out, rim_in,
    send1_sem, recv1_sem, send2_sem, recv2_sem, near_sem, rim_send_sem, rim_recv_sem,
):
    g, d = lax.axis_index("grp"), lax.axis_index("dev")
    y, x, core = d // 8, (d // 2) % 4, d % 2

    def far_first(items):
        return sorted(items, key=lambda m: -(min(m[0], 4 - m[0]) + min(m[1], 4 - m[1])))

    moves = far_first(
        [(dy, dx, dc) for dy in range(4) for dx in range(4) for dc in range(2) if dy or dx or dc]
    )
    peers = [
        (lax.rem(y + dy, 4) * 4 + lax.rem(x + dx, 4)) * 2 + lax.rem(core + dc, 2)
        for dy, dx, dc in moves
    ]

    barrier = pltpu.get_barrier_semaphore()
    for step in [s for n in range(NEAR, 0, -1) for s in (n, GRP - n)]:
        pl.semaphore_signal(
            barrier, 1, device_id={"grp": lax.rem(g + step, GRP), "dev": d}, device_id_type=MESH
        )
    for peer in peers:
        pl.semaphore_signal(barrier, 1, device_id={"grp": g, "dev": peer}, device_id_type=MESH)

    packed = pack(pos_ref[...], frc_ref[...], vol_ref[...], bin_ref[...], elem_ref[...])
    send1[...] = packed.reshape(send1.shape)
    acc[...] = jnp.zeros_like(acc)
    recv1[d] = send1[d]

    pl.semaphore_wait(barrier, 2 * NEAR + DEV - 1)
    for step in (NEAR, GRP - NEAR):
        pl.semaphore_signal(
            near_sem, 1, device_id={"grp": lax.rem(g + step, GRP), "dev": d}, device_id_type=MESH
        )
    for peer in peers:
        pltpu.make_async_remote_copy(
            src_ref=send1.at[peer],
            dst_ref=recv1.at[d],
            send_sem=send1_sem,
            recv_sem=recv1_sem,
            device_id={"grp": g, "dev": peer},
            device_id_type=MESH,
        ).start()
    others = recv1.at[pl.ds(0, DEV - 1)]
    pltpu.make_async_copy(others, others, recv1_sem).wait()

    arrived = recv1[...].reshape(16, 8, TILE)
    tiles = to_group_tiles([arrived[v] for v in range(16)])
    for v in range(16):
        send2[v] = tiles[v]
    recv2[g] = send2[g]

    pl.semaphore_wait(near_sem, 2)
    for step in [8] + [s for n in range(7, 0, -1) for s in (n, GRP - n)]:
        to = lax.rem(g + step, GRP)
        pltpu.make_async_remote_copy(
            src_ref=send2.at[to],
            dst_ref=recv2.at[g],
            send_sem=send2_sem,
            recv_sem=recv2_sem.at[step],
            device_id={"grp": to, "dev": d},
            device_id_type=MESH,
        ).start()

    def await_step(step):
        source = lax.rem(g - step + GRP, GRP)
        pltpu.make_async_copy(recv2.at[source], recv2.at[source], recv2_sem.at[step]).wait()
        return recv2[source]

    def body(n, carry):
        pair = jnp.concatenate([await_step(n), await_step(GRP - n)], axis=1)
        scaled, w_t, onehot = weigh(pair)
        for k in range(6):
            acc[k] += slab(scaled, w_t, onehot, k)
        return carry

    lax.fori_loop(1, 8, body, 0)

    pair = jnp.concatenate([recv2[g], await_step(8)], axis=1)
    scaled, w_t, onehot = weigh(pair)
    sub, lane = iota((8, TILE), 0), iota((8, TILE), 1)
    raw0 = acc[0] + slab(scaled, w_t, onehot, 0)
    raw5 = acc[5] + slab(scaled, w_t, onehot, 5)
    to_prev, to_next = jnp.zeros((8, TILE), F32), jnp.zeros((8, TILE), F32)
    for b in range(18):
        to_prev = jnp.where(lane == b, roll(raw0[8 * b:8 * b + 8], b, 1), to_prev)
        to_next = jnp.where(lane == b, roll(raw5[8 * b:8 * b + 8], b + 1, 1), to_next)
    rim_out[0] = to_prev
    rim_out[1] = to_next
    me = g * DEV + d
    ends = []
    for way, step in ((0, GRP * DEV - 1), (1, 1)):
        to = lax.rem(me + step, GRP * DEV)
        end = pltpu.make_async_remote_copy(
            src_ref=rim_out.at[way],
            dst_ref=rim_in.at[way],
            send_sem=rim_send_sem.at[way],
            recv_sem=rim_recv_sem.at[way],
            device_id={"grp": to // DEV, "dev": lax.rem(to, DEV)},
            device_id_type=MESH,
        )
        end.start()
        ends.append(end)

    for k in range(1, 5):
        out_ref[pl.ds(k, 144, stride=6), :] = acc[k] + slab(scaled, w_t, onehot, k)

    for end in ends:
        end.wait()
    from_next = jnp.where(me == GRP * DEV - 1, 0.0, rim_in[0])
    from_prev = jnp.where(me == 0, 0.0, rim_in[1])
    out5, out0 = [], []
    for b in range(18):
        block0, block5 = raw0[8 * b:8 * b + 8], raw5[8 * b:8 * b + 8]
        after = jnp.where(lane == TILE - 1, roll(from_next, TILE - 1 - b, 1), roll(block0, -1, 1))
        before = jnp.where(lane == 0, roll(from_prev, -b, 1), roll(block5, 1, 1))
        out5.append(block5 + after)
        out0.append(block0 + before)
    out_ref[pl.ds(0, 144, stride=6), :] = jnp.concatenate(out0, axis=0)
    out_ref[pl.ds(5, 144, stride=6), :] = jnp.concatenate(out5, axis=0)

    sent1 = send1.at[pl.ds(0, DEV - 1)]
    pltpu.make_async_copy(sent1, sent1, send1_sem).wait()
    sent2 = send2.at[pl.ds(0, GRP - 1)]
    pltpu.make_async_copy(sent2, sent2, send2_sem).wait()


def per_device(positions, forces, volumes, dest_bin, element):
    vmem = pl.BlockSpec(memory_space=pltpu.VMEM)
    dma = pltpu.SemaphoreType.DMA
    out = pl.pallas_call(
        kernel,
        out_shape=jax.ShapeDtypeStruct((864, ELEMS), F32),
        in_specs=[vmem] * 5,
        out_specs=vmem,
        scratch_shapes=[
            pltpu.VMEM((DEV, 4, TILE), F32),
            pltpu.VMEM((DEV, 4, TILE), F32),
            pltpu.VMEM((GRP, 8, TILE), F32),
            pltpu.VMEM((GRP, 8, TILE), F32),
            pltpu.VMEM((6, 144, ELEMS), F32),
            pltpu.VMEM((2, 8, TILE), F32),
            pltpu.VMEM((2, 8, TILE), F32),
            dma, dma, dma, dma((GRP,)), pltpu.SemaphoreType.REGULAR, dma((2,)), dma((2,)),
        ],
        compiler_params=pltpu.CompilerParams(collective_id=0, has_side_effects=True),
        name="project",
    )(
        positions,
        forces,
        volumes.reshape(1, LOCAL),
        dest_bin.reshape(1, LOCAL),
        element.reshape(1, LOCAL),
    )
    return out.reshape(4, 216, ELEMS)


def solution(mesh):
    in_specs = (
        P(None, ("grp", "dev")),
        P(None, ("grp", "dev")),
        P(("grp", "dev")),
        P(("grp", "dev"), None),
        P(("grp", "dev")),
    )
    out_specs = P(None, None, ("grp", "dev"))
    return jax.shard_map(
        per_device, mesh=mesh, in_specs=in_specs, out_specs=out_specs, check_vma=False
    )
```

time: 136 us -> 34.2 us (0.25)
  the two profiles are of different devices: /device:TPU:32 before, /device:TPU:1 now
where the time goes in v1:
time: 34.2 us; the launch traced here: 34 us
  Pallas kernels  32.2 us (94%)
  local copies, waits for them, and re-layouts  1.8 us (5%)
    pallas_call x1, Pallas kernels, per_device(): pl.pallas_call(kernel, out_shape=jax.ShapeDtypeStruct((864, ELEMS), F32),...  32.2 us
    unnamed x1, local copies, waits for them, and re-layouts  1.8 us

profile of v1, /device:TPU:1, one launch (start us, length us, event | category | flops | bytes accessed | tf_op | source)
XLA Modules:
  0.0 34.0 jit_solution(2838326511928326825)
XLA Ops:
  0.0 32.2 %project.1 = f32[864,128]{1,0:T(8,128)} custom-call(f32[3,1024]{1,0:T(4,128)} %pos_ref.1, f32[3,1024]{1,0:T(4,128)} %frc_ref.1, f32[1,1024]{1,0:T(1,128)} %bitcast.5, s32[1,1024]{1,0:T(1,128)} %bitcast.6, s32[1,1024]{1,0:T(1,128)} %bitcast.7), custom_call_target="tpu_custom_call" | custom-call | tf_op jit(solution)/shard_map/project/pallas_call | solution.py:280
  32.2 1.8 %copy.7 = f32[4,216,128]{2,1,0:T(8,128)} copy(f32[4,216,128]{2,1,0:T(8,128)} %bitcast.4) | data formatting | bytes 884736

commit v2 on v1

--- a/solution.py
+++ b/solution.py
@@ -12,7 +12,7 @@
 
 GRP, DEV, SLOTS, LOCAL, ELEMS = 16, 32, 4, 1024, 128
 TILE = 128
-NEAR = 4
+HALF = 8
 
 gll_points = (
     -1.0,
@@ -61,35 +61,35 @@
 
 
 def pack(positions, forces, volumes, target, element):
-    code = (target // DEV) * SLOTS + rank_in_bin(target)
-    lane_of = iota((TILE, LOCAL), 0)
-    mine = (lane_of // 4) == target % DEV
-    sub = iota((8, LOCAL), 0) % 4
-    rows = (
-        (positions[0:1], positions[1:2], positions[2:3], element.astype(F32)),
-        (forces[0:1], forces[1:2], forces[2:3], volumes),
+    dev = target % DEV
+    code = (dev % 2) * 64 + (dev // 2) * SLOTS + rank_in_bin(target)
+    row_of = iota((TILE, LOCAL), 0)
+    mine = (row_of // 8) == target // DEV
+    sub = iota((8, LOCAL), 0)
+    parts = [positions[n:n + 1] for n in range(3)] + [element.astype(F32)]
+    parts += [forces[n:n + 1] for n in range(3)] + [volumes]
+    feats = parts[7]
+    for n in range(7):
+        feats = jnp.where(sub == n, parts[n], feats)
+    left = jnp.concatenate(
+        [
+            jnp.where(mine, jnp.concatenate([piece] * 16, axis=0), 0.0).astype(BF16)
+            for piece in pieces(feats)
+        ],
+        axis=0,
     )
-    out = None
-    for half, (f0, f1, f2, f3) in enumerate(rows):
-        feats = jnp.where(sub == 0, f0, jnp.where(sub == 1, f1, jnp.where(sub == 2, f2, f3)))
-        left = jnp.concatenate(
-            [
-                jnp.where(mine, jnp.concatenate([piece] * 16, axis=0), 0.0).astype(BF16)
-                for piece in pieces(feats)
-            ],
-            axis=0,
-        )
-        right = jnp.where(lane_of == code + half * 64, 1.0, 0.0).astype(BF16)
-        prod = dot_nt(left, right)
-        part = prod[0:128] + prod[128:256] + prod[256:384]
-        out = part if out is None else out + part
-    return out
-
-
-def to_group_tiles(tiles):
+    right = jnp.where(row_of == code, 1.0, 0.0).astype(BF16)
+    prod = dot_nt(left, right)
+    return prod[0:128] + prod[128:256] + prod[256:384]
+
+
+def swap_halves(x):
     sub, lane = iota((8, TILE), 0), iota((8, TILE), 1)
-    keep = (sub // 4) == (lane // 64)
-    tiles = [jnp.where(keep, x, roll(roll(x, 4, 0), 64, 1)) for x in tiles]
+    return jnp.where((sub // 4) == (lane // 64), x, roll(roll(x, 4, 0), 64, 1))
+
+
+def to_dev_tiles(tiles):
+    lane = iota((8, TILE), 1)
     for bit in range(4):
         step = 4 << bit
         low = (lane // step) % 2 == 0
@@ -100,7 +100,7 @@
                 new[v] = jnp.where(low, a, roll(b, step, 1))
                 new[v | (1 << bit)] = jnp.where(low, roll(a, -step, 1), b)
         tiles = new
-    return tiles
+    return [swap_halves(x) for x in tiles]
 
 
 def by_row(sub, labels, parts):
@@ -144,88 +144,169 @@
     return dot_nt(contrib, onehot)
 
 
+CHIPS = sorted(
+    [(dy, dx) for dy in range(4) for dx in range(4)],
+    key=lambda m: min(m[0], 4 - m[0]) + min(m[1], 4 - m[1]),
+)
+
+
+def table(values):
+    return sum(v << (2 * n) for n, v in enumerate(values))
+
+
 def kernel(
-    pos_ref, frc_ref, vol_ref, bin_ref, elem_ref, out_ref,
+    pos_hbm, frc_hbm, vol_hbm, bin_hbm, elem_hbm, out_ref,
+    pos_ref, frc_ref, vol_ref, bin_ref, elem_ref,
     send1, recv1, send2, recv2, acc, rim_out, rim_in,
-    send1_sem, recv1_sem, send2_sem, recv2_sem, near_sem, rim_send_sem, rim_recv_sem,
+    in_sem, send1_sem, recv1_sem, send2_sem, recv2_sem, late_sem, all_sem, dev_sem,
+    rim_send_sem, rim_recv_sem,
 ):
     g, d = lax.axis_index("grp"), lax.axis_index("dev")
     y, x, core = d // 8, (d // 2) % 4, d % 2
-
-    def far_first(items):
-        return sorted(items, key=lambda m: -(min(m[0], 4 - m[0]) + min(m[1], 4 - m[1])))
-
-    moves = far_first(
-        [(dy, dx, dc) for dy in range(4) for dx in range(4) for dc in range(2) if dy or dx or dc]
-    )
-    peers = [
-        (lax.rem(y + dy, 4) * 4 + lax.rem(x + dx, 4)) * 2 + lax.rem(core + dc, 2)
-        for dy, dx, dc in moves
-    ]
+    late = g // HALF
+
+    loads = []
+    for n, (src, dst) in enumerate((
+        (bin_hbm, bin_ref), (pos_hbm, pos_ref), (frc_hbm, frc_ref),
+        (vol_hbm, vol_ref), (elem_hbm, elem_ref),
+    )):
+        load = pltpu.make_async_copy(src, dst, in_sem.at[n])
+        load.start()
+        loads.append(load)
+
+    def device(dy, dx, dc):
+        return (lax.rem(y + dy, 4) * 4 + lax.rem(x + dx, 4)) * 2 + lax.rem(core + dc, 2)
+
+    def greet(sem, grp, dev):
+        pl.semaphore_signal(sem, 1, device_id={"grp": grp, "dev": dev}, device_id_type=MESH)
 
     barrier = pltpu.get_barrier_semaphore()
-    for step in [s for n in range(NEAR, 0, -1) for s in (n, GRP - n)]:
-        pl.semaphore_signal(
-            barrier, 1, device_id={"grp": lax.rem(g + step, GRP), "dev": d}, device_id_type=MESH
-        )
-    for peer in peers:
-        pl.semaphore_signal(barrier, 1, device_id={"grp": g, "dev": peer}, device_id_type=MESH)
-
+    row = [(0, dx, dc) for dx in (2, 1, 3, 0) for dc in range(2) if dx or dc]
+    column = [(dy, 0, 0) for dy in (2, 1, 3)]
+    for move in row + column:
+        greet(barrier, g, device(*move))
+
+    @pl.when(late == 0)
+    def _():
+        for step in [8] + [s for n in range(7, 0, -1) for s in (n, GRP - n)]:
+            greet(barrier, lax.rem(g + step, GRP), d)
+
+    for load in loads:
+        load.wait()
     packed = pack(pos_ref[...], frc_ref[...], vol_ref[...], bin_ref[...], elem_ref[...])
     send1[...] = packed.reshape(send1.shape)
-    acc[...] = jnp.zeros_like(acc)
-    recv1[d] = send1[d]
-
-    pl.semaphore_wait(barrier, 2 * NEAR + DEV - 1)
-    for step in (NEAR, GRP - NEAR):
-        pl.semaphore_signal(
-            near_sem, 1, device_id={"grp": lax.rem(g + step, GRP), "dev": d}, device_id_type=MESH
-        )
-    for peer in peers:
+
+    pl.semaphore_wait(barrier, len(row) + len(column) + HALF - 1 + late)
+
+    def send_grp(to):
         pltpu.make_async_remote_copy(
-            src_ref=send1.at[peer],
-            dst_ref=recv1.at[d],
+            src_ref=send1.at[to],
+            dst_ref=recv1.at[g],
             send_sem=send1_sem,
             recv_sem=recv1_sem,
-            device_id={"grp": g, "dev": peer},
-            device_id_type=MESH,
-        ).start()
-    others = recv1.at[pl.ds(0, DEV - 1)]
-    pltpu.make_async_copy(others, others, recv1_sem).wait()
-
-    arrived = recv1[...].reshape(16, 8, TILE)
-    tiles = to_group_tiles([arrived[v] for v in range(16)])
-    for v in range(16):
-        send2[v] = tiles[v]
-    recv2[g] = send2[g]
-
-    pl.semaphore_wait(near_sem, 2)
-    for step in [8] + [s for n in range(7, 0, -1) for s in (n, GRP - n)]:
-        to = lax.rem(g + step, GRP)
-        pltpu.make_async_remote_copy(
-            src_ref=send2.at[to],
-            dst_ref=recv2.at[g],
-            send_sem=send2_sem,
-            recv_sem=recv2_sem.at[step],
             device_id={"grp": to, "dev": d},
             device_id_type=MESH,
         ).start()
 
-    def await_step(step):
-        source = lax.rem(g - step + GRP, GRP)
-        pltpu.make_async_copy(recv2.at[source], recv2.at[source], recv2_sem.at[step]).wait()
-        return recv2[source]
-
-    def body(n, carry):
-        pair = jnp.concatenate([await_step(n), await_step(GRP - n)], axis=1)
+    def send_own_half():
+        for step in range(1, HALF):
+            send_grp(late * HALF + lax.rem(g + step, HALF))
+
+    def send_other_half():
+        for n in range(HALF):
+            send_grp((1 - late) * HALF + n)
+
+    @pl.when(late == 0)
+    def _():
+        send_own_half()
+
+    @pl.when(late == 1)
+    def _():
+        send_other_half()
+        for n in range(HALF):
+            greet(late_sem, n, d)
+
+    for move in column:
+        greet(dev_sem, g, device(*move))
+    acc[...] = jnp.zeros_like(acc)
+    recv1[g] = send1[g]
+
+    @pl.when(late == 0)
+    def _():
+        pl.semaphore_wait(late_sem, HALF)
+
+        @pl.when(g == 0)
+        def _():
+            for n in range(HALF // 2):
+                greet(all_sem, GRP - 1 - n, d)
+
+        @pl.when(g == HALF - 1)
+        def _():
+            for n in range(HALF // 2):
+                greet(all_sem, HALF + n, d)
+
+        send_other_half()
+
+    @pl.when(late == 1)
+    def _():
+        pl.semaphore_wait(all_sem, 1)
+        send_own_half()
+
+    pl.semaphore_wait(dev_sem, len(column))
+    others = recv1.at[pl.ds(0, GRP - 1)]
+    pltpu.make_async_copy(others, others, recv1_sem).wait()
+
+    tiles = to_dev_tiles([recv1[v] for v in range(16)])
+    send2[...] = jnp.concatenate(tiles, axis=0).reshape(send2.shape)
+    for n in range(15, -1, -1):
+        dy, dx = CHIPS[n]
+        for dc in range(2):
+            if n or dc:
+                peer = device((4 - dy) % 4, (4 - dx) % 4, dc)
+                pltpu.make_async_remote_copy(
+                    src_ref=send2.at[peer],
+                    dst_ref=recv2.at[d],
+                    send_sem=send2_sem,
+                    recv_sem=recv2_sem.at[n // 2],
+                    device_id={"grp": g, "dev": peer},
+                    device_id_type=MESH,
+                ).start()
+    recv2[d] = send2[d]
+
+    def chip_tile(n, of):
+        shift = 2 * n
+        dy = (table([m[0] for m in CHIPS[of::2]]) >> shift) % 4
+        dx = (table([m[1] for m in CHIPS[of::2]]) >> shift) % 4
+        first = (lax.rem(y + dy, 4) * 4 + lax.rem(x + dx, 4)) * 2
+        return swap_halves(recv2[pl.ds(first, 2)].reshape(8, TILE))
+
+    def chunk(n, count):
+        part = recv2.at[pl.ds(0, count)]
+        pltpu.make_async_copy(part, part, recv2_sem.at[n]).wait()
+        return jnp.concatenate([chip_tile(n, 0), chip_tile(n, 1)], axis=1)
+
+    def add_chunk(pair):
         scaled, w_t, onehot = weigh(pair)
         for k in range(6):
             acc[k] += slab(scaled, w_t, onehot, k)
+
+    def body(n, carry):
+        @pl.when(n == 0)
+        def _():
+            part = recv2.at[pl.ds(0, 3)]
+            pltpu.make_async_copy(part, part, recv2_sem.at[n]).wait()
+
+        @pl.when(n > 0)
+        def _():
+            part = recv2.at[pl.ds(0, 4)]
+            pltpu.make_async_copy(part, part, recv2_sem.at[n]).wait()
+
+        add_chunk(jnp.concatenate([chip_tile(n, 0), chip_tile(n, 1)], axis=1))
         return carry
 
-    lax.fori_loop(1, 8, body, 0)
-
-    pair = jnp.concatenate([recv2[g], await_step(8)], axis=1)
+    lax.fori_loop(0, 7, body, 0)
+
+    pair = chunk(7, 4)
     scaled, w_t, onehot = weigh(pair)
     sub, lane = iota((8, TILE), 0), iota((8, TILE), 1)
     raw0 = acc[0] + slab(scaled, w_t, onehot, 0)
@@ -268,29 +349,35 @@
     out_ref[pl.ds(0, 144, stride=6), :] = jnp.concatenate(out0, axis=0)
     out_ref[pl.ds(5, 144, stride=6), :] = jnp.concatenate(out5, axis=0)
 
-    sent1 = send1.at[pl.ds(0, DEV - 1)]
+    sent1 = send1.at[pl.ds(0, GRP - 1)]
     pltpu.make_async_copy(sent1, sent1, send1_sem).wait()
-    sent2 = send2.at[pl.ds(0, GRP - 1)]
+    sent2 = send2.at[pl.ds(0, DEV - 1)]
     pltpu.make_async_copy(sent2, sent2, send2_sem).wait()
 
 
 def per_device(positions, forces, volumes, dest_bin, element):
     vmem = pl.BlockSpec(memory_space=pltpu.VMEM)
-    dma = pltpu.SemaphoreType.DMA
+    dma, regular = pltpu.SemaphoreType.DMA, pltpu.SemaphoreType.REGULAR
     out = pl.pallas_call(
         kernel,
         out_shape=jax.ShapeDtypeStruct((864, ELEMS), F32),
-        in_specs=[vmem] * 5,
+        in_specs=[pl.BlockSpec(memory_space=pl.ANY)] * 5,
         out_specs=vmem,
         scratch_shapes=[
+            pltpu.VMEM((3, LOCAL), F32),
+            pltpu.VMEM((3, LOCAL), F32),
+            pltpu.VMEM((1, LOCAL), F32),
+            pltpu.VMEM((1, LOCAL), I32),
+            pltpu.VMEM((1, LOCAL), I32),
+            pltpu.VMEM((GRP, 8, TILE), F32),
+            pltpu.VMEM((GRP, 8, TILE), F32),
             pltpu.VMEM((DEV, 4, TILE), F32),
             pltpu.VMEM((DEV, 4, TILE), F32),
-            pltpu.VMEM((GRP, 8, TILE), F32),
-            pltpu.VMEM((GRP, 8, TILE), F32),
             pltpu.VMEM((6, 144, ELEMS), F32),
             pltpu.VMEM((2, 8, TILE), F32),
             pltpu.VMEM((2, 8, TILE), F32),
-            dma, dma, dma, dma((GRP,)), pltpu.SemaphoreType.REGULAR, dma((2,)), dma((2,)),
+            dma((5,)), dma, dma, dma, dma((8,)), regular, regular, regular,
+            dma((2,)), dma((2,)),
         ],
         compiler_params=pltpu.CompilerParams(collective_id=0, has_side_effects=True),
         name="project",

time: 34.2 us -> 38 us (1.11)
  the two profiles are of different devices: /device:TPU:1 before, /device:TPU:0 now
where the time goes in v2:
time: 38 us; the launch traced here: 37.8 us
  Pallas kernels  36 us (95%)
  local copies, waits for them, and re-layouts  1.8 us (5%)
    pallas_call x1, Pallas kernels, per_device(): pl.pallas_call(kernel, out_shape=jax.ShapeDtypeStruct((864, ELEMS), F32),...  36 us
    unnamed x1, local copies, waits for them, and re-layouts  1.8 us

profile of v2, /device:TPU:0, one launch (start us, length us, event | category | flops | bytes accessed | tf_op | source)
XLA Modules:
  0.0 37.8 jit_solution(5126995783151613006)
XLA Ops:
  0.0 36.0 %project.1 = f32[864,128]{1,0:T(8,128)} custom-call(f32[3,1024]{1,0:T(4,128)} %pos_hbm.1, f32[3,1024]{1,0:T(4,128)} %frc_hbm.1, f32[1,1024]{1,0:T(1,128)} %bitcast.5, s32[1,1024]{1,0:T(1,128)} %bitcast.6, s32[1,1024]{1,0:T(1,128)} %bitcast.7), custom_call_target="tpu_custom_call" | custom-call | tf_op jit(solution)/shard_map/project/pallas_call | solution.py:361
  36.0 1.8 %copy.7 = f32[4,216,128]{2,1,0:T(8,128)} copy(f32[4,216,128]{2,1,0:T(8,128)} %bitcast.4) | data formatting | bytes 884736

commit v3 on v2

--- a/solution.py
+++ b/solution.py
@@ -138,10 +138,13 @@
     return scaled, w_t, onehot
 
 
-def slab(scaled, w_t, onehot, k):
-    weight = jnp.broadcast_to(w_t[k:k + 1], scaled[0].shape)
-    contrib = jnp.concatenate([part * weight for part in scaled], axis=0).astype(BF16)
-    return dot_nt(contrib, onehot)
+def slabs(x):
+    scaled, w_t, onehot = weigh(x)
+    rows = []
+    for k in range(6):
+        weight = jnp.broadcast_to(w_t[k:k + 1], scaled[0].shape)
+        rows += [part * weight for part in scaled]
+    return dot_nt(jnp.concatenate(rows, axis=0).astype(BF16), onehot)
 
 
 CHIPS = sorted(
@@ -150,15 +153,11 @@
 )
 
 
-def table(values):
-    return sum(v << (2 * n) for n, v in enumerate(values))
-
-
 def kernel(
     pos_hbm, frc_hbm, vol_hbm, bin_hbm, elem_hbm, out_ref,
     pos_ref, frc_ref, vol_ref, bin_ref, elem_ref,
     send1, recv1, send2, recv2, acc, rim_out, rim_in,
-    in_sem, send1_sem, recv1_sem, send2_sem, recv2_sem, late_sem, all_sem, dev_sem,
+    in_sem, send1_sem, recv1_sem, send2_sem, recv2_sem, late_sem, near_sem, far_sem, dev_sem,
     rim_send_sem, rim_recv_sem,
 ):
     g, d = lax.axis_index("grp"), lax.axis_index("dev")
@@ -191,12 +190,22 @@
         for step in [8] + [s for n in range(7, 0, -1) for s in (n, GRP - n)]:
             greet(barrier, lax.rem(g + step, GRP), d)
 
+    def for_late(deltas, act):
+        for delta in deltas:
+            @pl.when((late == 1) & (g + delta >= HALF) & (g + delta < GRP))
+            def _(delta=delta):
+                act(g + delta)
+
+    for_late((-2, 2, -1, 1), lambda to: greet(barrier, to, d))
+
     for load in loads:
         load.wait()
     packed = pack(pos_ref[...], frc_ref[...], vol_ref[...], bin_ref[...], elem_ref[...])
     send1[...] = packed.reshape(send1.shape)
 
-    pl.semaphore_wait(barrier, len(row) + len(column) + HALF - 1 + late)
+    below, above = g - HALF, GRP - 1 - g
+    greeted = late * (1 + jnp.minimum(below, 2) + jnp.minimum(above, 2))
+    pl.semaphore_wait(barrier, len(row) + len(column) + HALF - 1 + greeted)
 
     def send_grp(to):
         pltpu.make_async_remote_copy(
@@ -208,24 +217,20 @@
             device_id_type=MESH,
         ).start()
 
-    def send_own_half():
+    @pl.when(late == 0)
+    def _():
         for step in range(1, HALF):
-            send_grp(late * HALF + lax.rem(g + step, HALF))
-
-    def send_other_half():
+            send_grp(lax.rem(g + step, HALF))
+
+    @pl.when(late == 1)
+    def _():
         for n in range(HALF):
-            send_grp((1 - late) * HALF + n)
-
-    @pl.when(late == 0)
-    def _():
-        send_own_half()
-
-    @pl.when(late == 1)
-    def _():
-        send_other_half()
+            send_grp(n)
         for n in range(HALF):
             greet(late_sem, n, d)
 
+    for_late((-2, 2), lambda to: greet(near_sem, to, d))
+    for_late((-2, 2, -1, 1), send_grp)
     for move in column:
         greet(dev_sem, g, device(*move))
     acc[...] = jnp.zeros_like(acc)
@@ -234,23 +239,21 @@
     @pl.when(late == 0)
     def _():
         pl.semaphore_wait(late_sem, HALF)
-
-        @pl.when(g == 0)
-        def _():
-            for n in range(HALF // 2):
-                greet(all_sem, GRP - 1 - n, d)
-
-        @pl.when(g == HALF - 1)
-        def _():
-            for n in range(HALF // 2):
-                greet(all_sem, HALF + n, d)
-
-        send_other_half()
+        for n in range(HALF):
+            send_grp(HALF + n)
 
     @pl.when(late == 1)
     def _():
-        pl.semaphore_wait(all_sem, 1)
-        send_own_half()
+        pl.semaphore_wait(near_sem, jnp.minimum(below // 2, 1) + jnp.minimum(above // 2, 1))
+
+    for_late((-4, 4), lambda to: greet(far_sem, to, d))
+    for_late((-4, 4, -3, 3), send_grp)
+
+    @pl.when(late == 1)
+    def _():
+        pl.semaphore_wait(far_sem, 1)
+
+    for_late((-7, 7, -6, 6, -5, 5), send_grp)
 
     pl.semaphore_wait(dev_sem, len(column))
     others = recv1.at[pl.ds(0, GRP - 1)]
@@ -258,6 +261,7 @@
 
     tiles = to_dev_tiles([recv1[v] for v in range(16)])
     send2[...] = jnp.concatenate(tiles, axis=0).reshape(send2.shape)
+    slot = core * 16 + d // 2
     for n in range(15, -1, -1):
         dy, dx = CHIPS[n]
         for dc in range(2):
@@ -265,52 +269,44 @@
                 peer = device((4 - dy) % 4, (4 - dx) % 4, dc)
                 pltpu.make_async_remote_copy(
                     src_ref=send2.at[peer],
-                    dst_ref=recv2.at[d],
+                    dst_ref=recv2.at[slot],
                     send_sem=send2_sem,
-                    recv_sem=recv2_sem.at[n // 2],
+                    recv_sem=recv2_sem.at[(1 - core) * (1 + n // 8)],
                     device_id={"grp": g, "dev": peer},
                     device_id_type=MESH,
                 ).start()
-    recv2[d] = send2[d]
-
-    def chip_tile(n, of):
-        shift = 2 * n
-        dy = (table([m[0] for m in CHIPS[of::2]]) >> shift) % 4
-        dx = (table([m[1] for m in CHIPS[of::2]]) >> shift) % 4
-        first = (lax.rem(y + dy, 4) * 4 + lax.rem(x + dx, 4)) * 2
-        return swap_halves(recv2[pl.ds(first, 2)].reshape(8, TILE))
-
-    def chunk(n, count):
+    recv2[slot] = send2[d]
+
+    def await_chunk(n, count):
         part = recv2.at[pl.ds(0, count)]
         pltpu.make_async_copy(part, part, recv2_sem.at[n]).wait()
-        return jnp.concatenate([chip_tile(n, 0), chip_tile(n, 1)], axis=1)
-
-    def add_chunk(pair):
-        scaled, w_t, onehot = weigh(pair)
-        for k in range(6):
-            acc[k] += slab(scaled, w_t, onehot, k)
-
-    def body(n, carry):
-        @pl.when(n == 0)
+
+    def await_others(n, count, mine):
+        @pl.when(mine)
         def _():
-            part = recv2.at[pl.ds(0, 3)]
-            pltpu.make_async_copy(part, part, recv2_sem.at[n]).wait()
-
-        @pl.when(n > 0)
+            await_chunk(n, count - 1)
+
+        @pl.when(jnp.logical_not(mine))
         def _():
-            part = recv2.at[pl.ds(0, 4)]
-            pltpu.make_async_copy(part, part, recv2_sem.at[n]).wait()
-
-        add_chunk(jnp.concatenate([chip_tile(n, 0), chip_tile(n, 1)], axis=1))
-        return carry
-
-    lax.fori_loop(0, 7, body, 0)
-
-    pair = chunk(7, 4)
-    scaled, w_t, onehot = weigh(pair)
+            await_chunk(n, count)
+
+    def near(n):
+        dy, dx = CHIPS[n]
+        return recv2[lax.rem(y + dy, 4) * 4 + lax.rem(x + dx, 4)]
+
+    def project(pairs):
+        tiles = [swap_halves(jnp.concatenate(pair, axis=0)) for pair in pairs]
+        return slabs(jnp.concatenate(tiles, axis=1))
+
+    await_others(0, 16, core == 1)
+    acc[...] = project([(recv2[16 + n], recv2[17 + n]) for n in range(0, 16, 2)])
+    await_others(1, 8, core == 0)
+    acc[...] += project([(near(n), near(n + 1)) for n in range(0, 8, 2)])
+    await_chunk(2, 8)
+    raw = acc[...] + project([(near(n), near(n + 1)) for n in range(8, 16, 2)])
+    raw0, raw5 = raw[0:144], raw[720:864]
+    out_ref[144:720, :] = raw[144:720]
     sub, lane = iota((8, TILE), 0), iota((8, TILE), 1)
-    raw0 = acc[0] + slab(scaled, w_t, onehot, 0)
-    raw5 = acc[5] + slab(scaled, w_t, onehot, 5)
     to_prev, to_next = jnp.zeros((8, TILE), F32), jnp.zeros((8, TILE), F32)
     for b in range(18):
         to_prev = jnp.where(lane == b, roll(raw0[8 * b:8 * b + 8], b, 1), to_prev)
@@ -332,9 +328,6 @@
         end.start()
         ends.append(end)
 
-    for k in range(1, 5):
-        out_ref[pl.ds(k, 144, stride=6), :] = acc[k] + slab(scaled, w_t, onehot, k)
-
     for end in ends:
         end.wait()
     from_next = jnp.where(me == GRP * DEV - 1, 0.0, rim_in[0])
@@ -346,8 +339,8 @@
         before = jnp.where(lane == 0, roll(from_prev, -b, 1), roll(block5, 1, 1))
         out5.append(block5 + after)
         out0.append(block0 + before)
-    out_ref[pl.ds(0, 144, stride=6), :] = jnp.concatenate(out0, axis=0)
-    out_ref[pl.ds(5, 144, stride=6), :] = jnp.concatenate(out5, axis=0)
+    out_ref[0:144, :] = jnp.concatenate(out0, axis=0)
+    out_ref[720:864, :] = jnp.concatenate(out5, axis=0)
 
     sent1 = send1.at[pl.ds(0, GRP - 1)]
     pltpu.make_async_copy(sent1, sent1, send1_sem).wait()
@@ -355,12 +348,17 @@
     pltpu.make_async_copy(sent2, sent2, send2_sem).wait()
 
 
+def interleave(raw_ref, out_ref):
+    for k in range(6):
+        out_ref[pl.ds(k, 144, stride=6), :] = raw_ref[pl.ds(144 * k, 144), :]
+
+
 def per_device(positions, forces, volumes, dest_bin, element):
     vmem = pl.BlockSpec(memory_space=pltpu.VMEM)
     dma, regular = pltpu.SemaphoreType.DMA, pltpu.SemaphoreType.REGULAR
-    out = pl.pallas_call(
+    raw = pl.pallas_call(
         kernel,
-        out_shape=jax.ShapeDtypeStruct((864, ELEMS), F32),
+        out_shape=pltpu.VMEM((864, ELEMS), F32),
         in_specs=[pl.BlockSpec(memory_space=pl.ANY)] * 5,
         out_specs=vmem,
         scratch_shapes=[
@@ -373,10 +371,10 @@
             pltpu.VMEM((GRP, 8, TILE), F32),
             pltpu.VMEM((DEV, 4, TILE), F32),
             pltpu.VMEM((DEV, 4, TILE), F32),
-            pltpu.VMEM((6, 144, ELEMS), F32),
+            pltpu.VMEM((864, ELEMS), F32),
             pltpu.VMEM((2, 8, TILE), F32),
             pltpu.VMEM((2, 8, TILE), F32),
-            dma((5,)), dma, dma, dma, dma((8,)), regular, regular, regular,
+            dma((5,)), dma, dma, dma, dma((3,)), regular, regular, regular, regular,
             dma((2,)), dma((2,)),
         ],
         compiler_params=pltpu.CompilerParams(collective_id=0, has_side_effects=True),
@@ -388,6 +386,13 @@
         dest_bin.reshape(1, LOCAL),
         element.reshape(1, LOCAL),
     )
+    out = pl.pallas_call(
+        interleave,
+        out_shape=jax.ShapeDtypeStruct((864, ELEMS), F32),
+        in_specs=[vmem],
+        out_specs=vmem,
+        name="interleave",
+    )(pltpu.with_memory_space_constraint(raw, pltpu.VMEM))
     return out.reshape(4, 216, ELEMS)
 
 

time: 38 us -> 33.6 us (0.88)
  Pallas kernels: 36 us -> 33.4 us
  local copies, waits for them, and re-layouts: 1.8 us -> 0 us
    pallas_call x1 -> x2, Pallas kernels: 36 us -> 33.4 us  [the longest x1 32.6 us: per_device(): pl.pallas_call(kernel, out_shape=pltpu.VMEM((864, ELEMS), F32), in_specs=...]
    unnamed x1 -> x0, local copies, waits for them, and re-layouts: 1.8 us -> none
where the time goes in v3:
time: 33.6 us; the launch traced here: 33.4 us
  Pallas kernels  33.4 us (99%)
    pallas_call x1, Pallas kernels, per_device(): pl.pallas_call(kernel, out_shape=pltpu.VMEM((864, ELEMS), F32), in_specs=...  32.6 us
    pallas_call x1, Pallas kernels, per_device(): pl.pallas_call(interleave, out_shape=jax.ShapeDtypeStruct((864, ELEMS), F...  0.79 us

profile of v3, /device:TPU:0, one launch (start us, length us, event | category | flops | bytes accessed | tf_op | source)
XLA Modules:
  0.0 33.4 jit_solution(1056711428568729694)
XLA Ops:
  0.0 32.6 %project.1.raw_ref = f32[864,128]{1,0:T(8,128)S(1)} custom-call(f32[3,1024]{1,0:T(4,128)} %pos_hbm.1, f32[3,1024]{1,0:T(4,128)} %frc_hbm.1, f32[1,1024]{1,0:T(1,128)} %bitcast.4, s32[1,1024]{1,0:T(1,128)} %bitcast.5, s32[1,1024]{1,0:T(1,128)} %bitcast.6), custom_call_target="tpu_custom_call" | custom-call | tf_op jit(solution)/shard_map/project/pallas_call | solution.py:359
  32.6 0.8 %interleave.1 = f32[864,128]{1,0:T(8,128)} custom-call(f32[864,128]{1,0:T(8,128)S(1)} %project.1.raw_ref), custom_call_target="tpu_custom_call" | custom-call | tf_op jit(solution)/shard_map/interleave/pallas_call | solution.py:389

commit v4 on v3

--- a/solution.py
+++ b/solution.py
@@ -134,12 +134,12 @@
         by_row(sub, [(8 * b + s) // 36 for s in range(8)], values) * faces[b % 9]
         for b in range(18)
     ]
-    onehot = jnp.where(iota((ELEMS, width), 0) == x[3:4].astype(I32), 1.0, 0.0).astype(BF16)
-    return scaled, w_t, onehot
+    return scaled, w_t
 
 
 def slabs(x):
-    scaled, w_t, onehot = weigh(x)
+    scaled, w_t = weigh(x)
+    onehot = jnp.where(iota((ELEMS, x.shape[1]), 0) == x[3:4].astype(I32), 1.0, 0.0).astype(BF16)
     rows = []
     for k in range(6):
         weight = jnp.broadcast_to(w_t[k:k + 1], scaled[0].shape)
@@ -147,6 +147,36 @@
     return dot_nt(jnp.concatenate(rows, axis=0).astype(BF16), onehot)
 
 
+def face_sums(tiles):
+    x = jnp.concatenate(tiles, axis=1)
+    scaled, w_t = weigh(x)
+    first, last = x[3:4] == 0.0, x[3:4] == ELEMS - 1.0
+    weight = jnp.where(first, w_t[0:1], jnp.where(last, w_t[5:6], 0.0))
+    weight = jnp.broadcast_to(weight, scaled[0].shape)
+    rows = [part * weight for part in scaled]
+    fill = [jnp.zeros_like(weight)] * 7
+    rank, lane = iota((TILE, TILE), 0), iota((TILE, TILE), 1)
+    owner = ((lane // 4) % 16) * 2 + lane // 64
+    side = rank % 2
+    match = owner == (rank // 4 + 1 + 30 * side) % DEV
+    firsts, lasts = jnp.where(first, 1.0, 0.0), jnp.where(last, 1.0, 0.0)
+    chosen = jnp.concatenate(
+        [
+            jnp.where(
+                match & (side == 0),
+                firsts[:, t:t + TILE],
+                jnp.where(match & (side == 1), lasts[:, t:t + TILE], 0.0),
+            )
+            for t in range(0, x.shape[1], TILE)
+        ],
+        axis=1,
+    ).astype(BF16)
+    halves = [
+        dot_nt(chosen, jnp.concatenate(rows[h:h + 9] + fill, axis=0).astype(BF16)) for h in (0, 9)
+    ]
+    return jnp.where(rank % 4 < 2, halves[0], halves[1])
+
+
 CHIPS = sorted(
     [(dy, dx) for dy in range(4) for dx in range(4)],
     key=lambda m: min(m[0], 4 - m[0]) + min(m[1], 4 - m[1]),
@@ -156,9 +186,9 @@
 def kernel(
     pos_hbm, frc_hbm, vol_hbm, bin_hbm, elem_hbm, out_ref,
     pos_ref, frc_ref, vol_ref, bin_ref, elem_ref,
-    send1, recv1, send2, recv2, acc, rim_out, rim_in,
+    send1, recv1, send2, recv2, acc, send3, recv3, recv3x, rim,
     in_sem, send1_sem, recv1_sem, send2_sem, recv2_sem, late_sem, near_sem, far_sem, dev_sem,
-    rim_send_sem, rim_recv_sem,
+    slab_sem, send3_sem, recv3_sem, send3x_sem, recv3x_sem,
 ):
     g, d = lax.axis_index("grp"), lax.axis_index("dev")
     y, x, core = d // 8, (d // 2) % 4, d % 2
@@ -233,7 +263,6 @@
     for_late((-2, 2, -1, 1), send_grp)
     for move in column:
         greet(dev_sem, g, device(*move))
-    acc[...] = jnp.zeros_like(acc)
     recv1[g] = send1[g]
 
     @pl.when(late == 0)
@@ -256,26 +285,67 @@
     for_late((-7, 7, -6, 6, -5, 5), send_grp)
 
     pl.semaphore_wait(dev_sem, len(column))
+
+    @pl.when(g > 0)
+    def _():
+        greet(slab_sem, g - 1, d)
+
+    @pl.when(g < GRP - 1)
+    def _():
+        greet(slab_sem, g + 1, d)
+
     others = recv1.at[pl.ds(0, GRP - 1)]
     pltpu.make_async_copy(others, others, recv1_sem).wait()
 
-    tiles = to_dev_tiles([recv1[v] for v in range(16)])
+    arrived = [recv1[v] for v in range(16)]
+    tiles = to_dev_tiles(arrived)
     send2[...] = jnp.concatenate(tiles, axis=0).reshape(send2.shape)
     slot = core * 16 + d // 2
-    for n in range(15, -1, -1):
-        dy, dx = CHIPS[n]
-        for dc in range(2):
-            if n or dc:
-                peer = device((4 - dy) % 4, (4 - dx) % 4, dc)
-                pltpu.make_async_remote_copy(
-                    src_ref=send2.at[peer],
-                    dst_ref=recv2.at[slot],
-                    send_sem=send2_sem,
-                    recv_sem=recv2_sem.at[(1 - core) * (1 + n // 8)],
-                    device_id={"grp": g, "dev": peer},
-                    device_id_type=MESH,
-                ).start()
+    others = [
+        (n, device((4 - CHIPS[n][0]) % 4, (4 - CHIPS[n][1]) % 4, dc))
+        for n in range(15, -1, -1) for dc in range(2) if n or dc
+    ]
+    for n, peer in others:
+        pltpu.make_async_remote_copy(
+            src_ref=send2.at[peer],
+            dst_ref=recv2.at[slot],
+            send_sem=send2_sem,
+            recv_sem=recv2_sem.at[(1 - core) * (1 + n // 8)],
+            device_id={"grp": g, "dev": peer},
+            device_id_type=MESH,
+        ).start()
     recv2[slot] = send2[d]
+
+    send3[...] = face_sums(arrived).reshape(send3.shape)
+    for _, peer in others:
+        pltpu.make_async_remote_copy(
+            src_ref=send3.at[peer],
+            dst_ref=recv3.at[d],
+            send_sem=send3_sem,
+            recv_sem=recv3_sem,
+            device_id={"grp": g, "dev": peer},
+            device_id_type=MESH,
+        ).start()
+    recv3[d] = send3[d]
+    pl.semaphore_wait(slab_sem, jnp.minimum(g, 1) + jnp.minimum(GRP - 1 - g, 1))
+
+    def to_slab(n, grp, dev):
+        return pltpu.make_async_remote_copy(
+            src_ref=send3.at[dev],
+            dst_ref=recv3x.at[d],
+            send_sem=send3x_sem.at[n],
+            recv_sem=recv3x_sem,
+            device_id={"grp": grp, "dev": dev},
+            device_id_type=MESH,
+        )
+
+    @pl.when(g > 0)
+    def _():
+        to_slab(0, g - 1, DEV - 1).start()
+
+    @pl.when(g < GRP - 1)
+    def _():
+        to_slab(1, g + 1, 0).start()
 
     def await_chunk(n, count):
         part = recv2.at[pl.ds(0, count)]
@@ -306,37 +376,34 @@
     raw = acc[...] + project([(near(n), near(n + 1)) for n in range(8, 16, 2)])
     raw0, raw5 = raw[0:144], raw[720:864]
     out_ref[144:720, :] = raw[144:720]
-    sub, lane = iota((8, TILE), 0), iota((8, TILE), 1)
-    to_prev, to_next = jnp.zeros((8, TILE), F32), jnp.zeros((8, TILE), F32)
-    for b in range(18):
-        to_prev = jnp.where(lane == b, roll(raw0[8 * b:8 * b + 8], b, 1), to_prev)
-        to_next = jnp.where(lane == b, roll(raw5[8 * b:8 * b + 8], b + 1, 1), to_next)
-    rim_out[0] = to_prev
-    rim_out[1] = to_next
-    me = g * DEV + d
-    ends = []
-    for way, step in ((0, GRP * DEV - 1), (1, 1)):
-        to = lax.rem(me + step, GRP * DEV)
-        end = pltpu.make_async_remote_copy(
-            src_ref=rim_out.at[way],
-            dst_ref=rim_in.at[way],
-            send_sem=rim_send_sem.at[way],
-            recv_sem=rim_recv_sem.at[way],
-            device_id={"grp": to // DEV, "dev": lax.rem(to, DEV)},
-            device_id_type=MESH,
-        )
-        end.start()
-        ends.append(end)
-
-    for end in ends:
-        end.wait()
-    from_next = jnp.where(me == GRP * DEV - 1, 0.0, rim_in[0])
-    from_prev = jnp.where(me == 0, 0.0, rim_in[1])
+
+    rest = recv3.at[pl.ds(0, DEV - 1)]
+    pltpu.make_async_copy(rest, rest, recv3_sem).wait()
+    side = iota((4, TILE), 0) % 2
+    keep = jnp.where(side == 0, jnp.minimum(DEV - 1 - d, 1), jnp.minimum(d, 1)).astype(F32)
+    rim[...] = jnp.zeros_like(rim)
+    rim[0:4, :] = keep * jnp.sum(recv3[...], axis=0)
+
+    def add_slab(of):
+        pltpu.make_async_copy(recv3x, recv3x, recv3x_sem).wait()
+        rim[0:4, :] += jnp.where(side == of, jnp.sum(recv3x[...], axis=0), 0.0)
+
+    @pl.when((d == DEV - 1) & (g < GRP - 1))
+    def _():
+        add_slab(0)
+
+    @pl.when((d == 0) & (g > 0))
+    def _():
+        add_slab(1)
+
+    columns = jnp.transpose(jnp.concatenate([rim[...], jnp.zeros((TILE - 8, TILE), F32)], axis=0))
+    lane = iota((8, TILE), 1)
     out5, out0 = [], []
     for b in range(18):
         block0, block5 = raw0[8 * b:8 * b + 8], raw5[8 * b:8 * b + 8]
-        after = jnp.where(lane == TILE - 1, roll(from_next, TILE - 1 - b, 1), roll(block0, -1, 1))
-        before = jnp.where(lane == 0, roll(from_prev, -b, 1), roll(block5, 1, 1))
+        faces, half = columns[8 * (b % 9):8 * (b % 9) + 8], 2 * (b // 9)
+        after = jnp.where(lane == TILE - 1, roll(faces, TILE - 1 - half, 1), roll(block0, -1, 1))
+        before = jnp.where(lane == 0, roll(faces, -1 - half, 1), roll(block5, 1, 1))
         out5.append(block5 + after)
         out0.append(block0 + before)
     out_ref[0:144, :] = jnp.concatenate(out0, axis=0)
@@ -346,6 +413,16 @@
     pltpu.make_async_copy(sent1, sent1, send1_sem).wait()
     sent2 = send2.at[pl.ds(0, DEV - 1)]
     pltpu.make_async_copy(sent2, sent2, send2_sem).wait()
+    sent3 = send3.at[pl.ds(0, DEV - 1)]
+    pltpu.make_async_copy(sent3, sent3, send3_sem).wait()
+
+    @pl.when(g > 0)
+    def _():
+        to_slab(0, g - 1, DEV - 1).wait_send()
+
+    @pl.when(g < GRP - 1)
+    def _():
+        to_slab(1, g + 1, 0).wait_send()
 
 
 def interleave(raw_ref, out_ref):
@@ -372,10 +449,12 @@
             pltpu.VMEM((DEV, 4, TILE), F32),
             pltpu.VMEM((DEV, 4, TILE), F32),
             pltpu.VMEM((864, ELEMS), F32),
-            pltpu.VMEM((2, 8, TILE), F32),
-            pltpu.VMEM((2, 8, TILE), F32),
+            pltpu.VMEM((DEV, 4, TILE), F32),
+            pltpu.VMEM((DEV, 4, TILE), F32),
+            pltpu.VMEM((DEV, 4, TILE), F32),
+            pltpu.VMEM((8, TILE), F32),
             dma((5,)), dma, dma, dma, dma((3,)), regular, regular, regular, regular,
-            dma((2,)), dma((2,)),
+            regular, dma, dma, dma((2,)), dma,
         ],
         compiler_params=pltpu.CompilerParams(collective_id=0, has_side_effects=True),
         name="project",

time: 33.6 us -> 28.8 us (0.86)
  the two profiles are of different devices: /device:TPU:0 before, /device:TPU:1 now
where the time goes in v4:
time: 28.8 us; the launch traced here: 28.6 us
  Pallas kernels  28.6 us (99%)
    pallas_call x1, Pallas kernels, per_device(): pl.pallas_call(kernel, out_shape=pltpu.VMEM((864, ELEMS), F32), in_specs=...  27.8 us
    pallas_call x1, Pallas kernels, per_device(): pl.pallas_call(interleave, out_shape=jax.ShapeDtypeStruct((864, ELEMS), F...  0.79 us

profile of v4, /device:TPU:1, one launch (start us, length us, event | category | flops | bytes accessed | tf_op | source)
XLA Modules:
  0.0 28.6 jit_solution(14430573720028144426)
XLA Ops:
  0.0 27.8 %project.1.raw_ref = f32[864,128]{1,0:T(8,128)S(1)} custom-call(f32[3,1024]{1,0:T(4,128)} %pos_hbm.1, f32[3,1024]{1,0:T(4,128)} %frc_hbm.1, f32[1,1024]{1,0:T(1,128)} %bitcast.4, s32[1,1024]{1,0:T(1,128)} %bitcast.5, s32[1,1024]{1,0:T(1,128)} %bitcast.6), custom_call_target="tpu_custom_call" | custom-call | tf_op jit(solution)/shard_map/project/pallas_call | solution.py:436
  27.8 0.8 %interleave.1 = f32[864,128]{1,0:T(8,128)} custom-call(f32[864,128]{1,0:T(8,128)S(1)} %project.1.raw_ref), custom_call_target="tpu_custom_call" | custom-call | tf_op jit(solution)/shard_map/interleave/pallas_call | solution.py:468

commit v5 on v4

--- a/solution.py
+++ b/solution.py
@@ -12,7 +12,8 @@
 
 GRP, DEV, SLOTS, LOCAL, ELEMS = 16, 32, 4, 1024, 128
 TILE = 128
-HALF = 8
+EARLY, LATE = 6, 10
+BOUNDS = (10,)
 
 gll_points = (
     -1.0,
@@ -187,12 +188,12 @@
     pos_hbm, frc_hbm, vol_hbm, bin_hbm, elem_hbm, out_ref,
     pos_ref, frc_ref, vol_ref, bin_ref, elem_ref,
     send1, recv1, send2, recv2, acc, send3, recv3, recv3x, rim,
-    in_sem, send1_sem, recv1_sem, send2_sem, recv2_sem, late_sem, near_sem, far_sem, dev_sem,
-    slab_sem, send3_sem, recv3_sem, send3x_sem, recv3x_sem,
+    in_sem, send1_sem, recv1_sem, send2_sem, recv2_sem, late_sem, near_sem,
+    slab_sem, chain_sem, send3_sem, recv3_sem, send3x_sem, recv3x_sem,
 ):
     g, d = lax.axis_index("grp"), lax.axis_index("dev")
     y, x, core = d // 8, (d // 2) % 4, d % 2
-    late = g // HALF
+    late = (g + LATE) // GRP
 
     loads = []
     for n, (src, dst) in enumerate((
@@ -209,98 +210,106 @@
     def greet(sem, grp, dev):
         pl.semaphore_signal(sem, 1, device_id={"grp": grp, "dev": dev}, device_id_type=MESH)
 
-    barrier = pltpu.get_barrier_semaphore()
+    other = d + 1 - 2 * core
+    below, above = g - EARLY, GRP - 1 - g
     row = [(0, dx, dc) for dx in (2, 1, 3, 0) for dc in range(2) if dx or dc]
-    column = [(dy, 0, 0) for dy in (2, 1, 3)]
-    for move in row + column:
-        greet(barrier, g, device(*move))
-
-    @pl.when(late == 0)
-    def _():
-        for step in [8] + [s for n in range(7, 0, -1) for s in (n, GRP - n)]:
-            greet(barrier, lax.rem(g + step, GRP), d)
+    column = [(2, 0, 0), (1, 0, 0), (3, 0, 0)]
+
+    def only(condition, act):
+        @pl.when(condition)
+        def _():
+            act()
+
+    def greet_moves(sem, moves):
+        for move in moves:
+            greet(sem, g, device(*move))
 
     def for_late(deltas, act):
         for delta in deltas:
-            @pl.when((late == 1) & (g + delta >= HALF) & (g + delta < GRP))
-            def _(delta=delta):
-                act(g + delta)
-
-    for_late((-2, 2, -1, 1), lambda to: greet(barrier, to, d))
+            inside = (late == 1) & (g + delta >= EARLY) & (g + delta < GRP)
+            only(inside, functools.partial(act, g + delta))
+
+    def greet_both(to):
+        greet(barrier, to, d)
+        greet(barrier, to, other)
+
+    def in_range(delta):
+        return jnp.minimum(below // delta, 1) + jnp.minimum(above // delta, 1)
+
+    barrier = pltpu.get_barrier_semaphore()
+
+    def greet_grp():
+        for n in range(EARLY):
+            only(g != n, functools.partial(greet, barrier, n, other))
+        for n in range(LATE):
+            greet(barrier, EARLY + n, other)
+
+    greet_moves(barrier, row + column)
+    for_late((-2, 2, -1, 1), greet_both)
+    only(late == 0, greet_grp)
 
     for load in loads:
         load.wait()
     packed = pack(pos_ref[...], frc_ref[...], vol_ref[...], bin_ref[...], elem_ref[...])
     send1[...] = packed.reshape(send1.shape)
 
-    below, above = g - HALF, GRP - 1 - g
-    greeted = late * (1 + jnp.minimum(below, 2) + jnp.minimum(above, 2))
-    pl.semaphore_wait(barrier, len(row) + len(column) + HALF - 1 + greeted)
+    greeted = EARLY - 1 + late * (1 + 2 * in_range(1) + 2 * in_range(2))
+    pl.semaphore_wait(barrier, len(row) + len(column) + greeted)
 
     def send_grp(to):
         pltpu.make_async_remote_copy(
             src_ref=send1.at[to],
             dst_ref=recv1.at[g],
             send_sem=send1_sem,
-            recv_sem=recv1_sem,
-            device_id={"grp": to, "dev": d},
+            recv_sem=recv1_sem.at[late],
+            device_id={"grp": to, "dev": other},
             device_id_type=MESH,
         ).start()
 
-    @pl.when(late == 0)
-    def _():
-        for step in range(1, HALF):
-            send_grp(lax.rem(g + step, HALF))
-
-    @pl.when(late == 1)
-    def _():
-        for n in range(HALF):
+    def early_sends():
+        for n in range(EARLY):
+            only(g != n, functools.partial(send_grp, n))
+        send_grp(g)
+        greet_moves(slab_sem, column)
+        pl.semaphore_wait(late_sem, LATE)
+        for n in range(LATE):
+            send_grp(EARLY + n)
+
+    def late_sends():
+        for n in range(EARLY):
             send_grp(n)
-        for n in range(HALF):
-            greet(late_sem, n, d)
-
-    for_late((-2, 2), lambda to: greet(near_sem, to, d))
-    for_late((-2, 2, -1, 1), send_grp)
-    for move in column:
-        greet(dev_sem, g, device(*move))
-    recv1[g] = send1[g]
-
-    @pl.when(late == 0)
-    def _():
-        pl.semaphore_wait(late_sem, HALF)
-        for n in range(HALF):
-            send_grp(HALF + n)
-
-    @pl.when(late == 1)
-    def _():
-        pl.semaphore_wait(near_sem, jnp.minimum(below // 2, 1) + jnp.minimum(above // 2, 1))
-
-    for_late((-4, 4), lambda to: greet(far_sem, to, d))
-    for_late((-4, 4, -3, 3), send_grp)
-
-    @pl.when(late == 1)
-    def _():
-        pl.semaphore_wait(far_sem, 1)
-
-    for_late((-7, 7, -6, 6, -5, 5), send_grp)
-
-    pl.semaphore_wait(dev_sem, len(column))
-
-    @pl.when(g > 0)
-    def _():
-        greet(slab_sem, g - 1, d)
-
-    @pl.when(g < GRP - 1)
-    def _():
-        greet(slab_sem, g + 1, d)
-
-    others = recv1.at[pl.ds(0, GRP - 1)]
-    pltpu.make_async_copy(others, others, recv1_sem).wait()
-
-    arrived = [recv1[v] for v in range(16)]
-    tiles = to_dev_tiles(arrived)
+        for n in range(EARLY):
+            greet(late_sem, n, other)
+        for_late((-2, 2), lambda to: greet(near_sem.at[0], to, d))
+        greet_moves(slab_sem, column)
+        for_late((-2, 2, -1, 1), send_grp)
+        send_grp(g)
+        pl.semaphore_wait(near_sem.at[0], in_range(2))
+        for_late((-4, 4), lambda to: greet(near_sem.at[1], to, d))
+        for_late((-4, 4, -3, 3), send_grp)
+        pl.semaphore_wait(near_sem.at[1], in_range(4))
+        only(g == EARLY + 1, lambda: greet(near_sem.at[2], EARLY, d))
+        only(g == GRP - 2, lambda: greet(near_sem.at[2], GRP - 1, d))
+        for_late((-8, 8, -7, 7, -6, 6, -5, 5), send_grp)
+        only((g == EARLY) | (g == GRP - 1), lambda: pl.semaphore_wait(near_sem.at[2], 1))
+        for_late((-9, 9), send_grp)
+
+    only(late == 0, early_sends)
+    only(late == 1, late_sends)
+    pl.semaphore_wait(slab_sem, len(column))
+
+    only(g > 0, lambda: greet(chain_sem, g - 1, other))
+    only(g < GRP - 1, lambda: greet(chain_sem, g + 1, other))
+
+    def await_grp(n, count):
+        part = recv1.at[pl.ds(0, count)]
+        pltpu.make_async_copy(part, part, recv1_sem.at[n]).wait()
+
+    await_grp(0, EARLY)
+    acc[0:TILE, :] = face_sums([recv1[v] for v in range(EARLY)])
+    await_grp(1, LATE)
+    tiles = to_dev_tiles([recv1[v] for v in range(GRP)])
     send2[...] = jnp.concatenate(tiles, axis=0).reshape(send2.shape)
-    slot = core * 16 + d // 2
     others = [
         (n, device((4 - CHIPS[n][0]) % 4, (4 - CHIPS[n][1]) % 4, dc))
         for n in range(15, -1, -1) for dc in range(2) if n or dc
@@ -308,15 +317,16 @@
     for n, peer in others:
         pltpu.make_async_remote_copy(
             src_ref=send2.at[peer],
-            dst_ref=recv2.at[slot],
+            dst_ref=recv2.at[d],
             send_sem=send2_sem,
-            recv_sem=recv2_sem.at[(1 - core) * (1 + n // 8)],
+            recv_sem=recv2_sem.at[sum(n >= b for b in BOUNDS)],
             device_id={"grp": g, "dev": peer},
             device_id_type=MESH,
         ).start()
-    recv2[slot] = send2[d]
-
-    send3[...] = face_sums(arrived).reshape(send3.shape)
+    recv2[d] = send2[d]
+
+    sums = acc[0:TILE, :] + face_sums([recv1[v] for v in range(EARLY, GRP)])
+    send3[...] = sums.reshape(send3.shape)
     for _, peer in others:
         pltpu.make_async_remote_copy(
             src_ref=send3.at[peer],
@@ -327,7 +337,7 @@
             device_id_type=MESH,
         ).start()
     recv3[d] = send3[d]
-    pl.semaphore_wait(slab_sem, jnp.minimum(g, 1) + jnp.minimum(GRP - 1 - g, 1))
+    pl.semaphore_wait(chain_sem, jnp.minimum(g, 1) + jnp.minimum(GRP - 1 - g, 1))
 
     def to_slab(n, grp, dev):
         return pltpu.make_async_remote_copy(
@@ -351,29 +361,20 @@
         part = recv2.at[pl.ds(0, count)]
         pltpu.make_async_copy(part, part, recv2_sem.at[n]).wait()
 
-    def await_others(n, count, mine):
-        @pl.when(mine)
-        def _():
-            await_chunk(n, count - 1)
-
-        @pl.when(jnp.logical_not(mine))
-        def _():
-            await_chunk(n, count)
-
-    def near(n):
+    def tile(n):
         dy, dx = CHIPS[n]
-        return recv2[lax.rem(y + dy, 4) * 4 + lax.rem(x + dx, 4)]
-
-    def project(pairs):
-        tiles = [swap_halves(jnp.concatenate(pair, axis=0)) for pair in pairs]
-        return slabs(jnp.concatenate(tiles, axis=1))
-
-    await_others(0, 16, core == 1)
-    acc[...] = project([(recv2[16 + n], recv2[17 + n]) for n in range(0, 16, 2)])
-    await_others(1, 8, core == 0)
-    acc[...] += project([(near(n), near(n + 1)) for n in range(0, 8, 2)])
-    await_chunk(2, 8)
-    raw = acc[...] + project([(near(n), near(n + 1)) for n in range(8, 16, 2)])
+        first = (lax.rem(y + dy, 4) * 4 + lax.rem(x + dx, 4)) * 2
+        return swap_halves(recv2[pl.ds(first, 2)].reshape(8, TILE))
+
+    def project(chips):
+        return slabs(jnp.concatenate([tile(n) for n in chips], axis=1))
+
+    raw = None
+    for part, (low, high) in enumerate(zip((0,) + BOUNDS, BOUNDS + (16,))):
+        await_chunk(part, 2 * (high - low) - (part == 0))
+        if raw is not None:
+            acc[...] = raw
+        raw = project(range(low, high)) + (0.0 if raw is None else acc[...])
     raw0, raw5 = raw[0:144], raw[720:864]
     out_ref[144:720, :] = raw[144:720]
 
@@ -409,8 +410,7 @@
     out_ref[0:144, :] = jnp.concatenate(out0, axis=0)
     out_ref[720:864, :] = jnp.concatenate(out5, axis=0)
 
-    sent1 = send1.at[pl.ds(0, GRP - 1)]
-    pltpu.make_async_copy(sent1, sent1, send1_sem).wait()
+    pltpu.make_async_copy(send1, send1, send1_sem).wait()
     sent2 = send2.at[pl.ds(0, DEV - 1)]
     pltpu.make_async_copy(sent2, sent2, send2_sem).wait()
     sent3 = send3.at[pl.ds(0, DEV - 1)]
@@ -453,8 +453,8 @@
             pltpu.VMEM((DEV, 4, TILE), F32),
             pltpu.VMEM((DEV, 4, TILE), F32),
             pltpu.VMEM((8, TILE), F32),
-            dma((5,)), dma, dma, dma, dma((3,)), regular, regular, regular, regular,
-            regular, dma, dma, dma((2,)), dma,
+            dma((5,)), dma, dma((2,)), dma, dma((1 + len(BOUNDS),)), regular, regular((3,)),
+            regular, regular, dma, dma, dma((2,)), dma,
         ],
         compiler_params=pltpu.CompilerParams(collective_id=0, has_side_effects=True),
         name="project",

time: 28.8 us -> 28.4 us (0.986)
  Pallas kernels: 28.6 us -> 28.2 us
    pallas_call x1, Pallas kernels: 27.8 us -> 27.4 us  [per_device(): pl.pallas_call(kernel, out_shape=pltpu.VMEM((864, ELEMS), F32), in_specs=...]
where the time goes in v5:
time: 28.4 us; the launch traced here: 28.2 us
  Pallas kernels  28.2 us (99%)
    pallas_call x1, Pallas kernels, per_device(): pl.pallas_call(kernel, out_shape=pltpu.VMEM((864, ELEMS), F32), in_specs=...  27.4 us
    pallas_call x1, Pallas kernels, per_device(): pl.pallas_call(interleave, out_shape=jax.ShapeDtypeStruct((864, ELEMS), F...  0.79 us

profile of v5, /device:TPU:1, one launch (start us, length us, event | category | flops | bytes accessed | tf_op | source)
XLA Modules:
  0.0 28.2 jit_solution(6949509985968208015)
XLA Ops:
  0.0 27.4 %project.1.raw_ref = f32[864,128]{1,0:T(8,128)S(1)} custom-call(f32[3,1024]{1,0:T(4,128)} %pos_hbm.1, f32[3,1024]{1,0:T(4,128)} %frc_hbm.1, f32[1,1024]{1,0:T(1,128)} %bitcast.4, s32[1,1024]{1,0:T(1,128)} %bitcast.5, s32[1,1024]{1,0:T(1,128)} %bitcast.6), custom_call_target="tpu_custom_call" | custom-call | tf_op jit(solution)/shard_map/project/pallas_call | solution.py:436
  27.4 0.8 %interleave.1 = f32[864,128]{1,0:T(8,128)} custom-call(f32[864,128]{1,0:T(8,128)S(1)} %project.1.raw_ref), custom_call_target="tpu_custom_call" | custom-call | tf_op jit(solution)/shard_map/interleave/pallas_call | solution.py:468

commit v6 on v5

--- a/solution.py
+++ b/solution.py
@@ -188,7 +188,7 @@
     pos_hbm, frc_hbm, vol_hbm, bin_hbm, elem_hbm, out_ref,
     pos_ref, frc_ref, vol_ref, bin_ref, elem_ref,
     send1, recv1, send2, recv2, acc, send3, recv3, recv3x, rim,
-    in_sem, send1_sem, recv1_sem, send2_sem, recv2_sem, late_sem, near_sem,
+    in_sem, send1_sem, recv1_sem, send2_sem, recv2_sem, late_sem, near_sem, row_sem, column_sem,
     slab_sem, chain_sem, send3_sem, recv3_sem, send3x_sem, recv3x_sem,
 ):
     g, d = lax.axis_index("grp"), lax.axis_index("dev")
@@ -212,8 +212,8 @@
 
     other = d + 1 - 2 * core
     below, above = g - EARLY, GRP - 1 - g
-    row = [(0, dx, dc) for dx in (2, 1, 3, 0) for dc in range(2) if dx or dc]
-    column = [(2, 0, 0), (1, 0, 0), (3, 0, 0)]
+    row = [(0, dx, dc) for dx in (1, 3, 0) for dc in range(2) if dx or dc]
+    beside, column = [(0, 1, 0), (0, 3, 0)], [(1, 0, 0), (3, 0, 0)]
 
     def only(condition, act):
         @pl.when(condition)
@@ -245,7 +245,7 @@
             greet(barrier, EARLY + n, other)
 
     greet_moves(barrier, row + column)
-    for_late((-2, 2, -1, 1), greet_both)
+    for_late((-1, 1), greet_both)
     only(late == 0, greet_grp)
 
     for load in loads:
@@ -253,7 +253,7 @@
     packed = pack(pos_ref[...], frc_ref[...], vol_ref[...], bin_ref[...], elem_ref[...])
     send1[...] = packed.reshape(send1.shape)
 
-    greeted = EARLY - 1 + late * (1 + 2 * in_range(1) + 2 * in_range(2))
+    greeted = EARLY - 1 + late * (1 + 2 * in_range(1))
     pl.semaphore_wait(barrier, len(row) + len(column) + greeted)
 
     def send_grp(to):
@@ -266,37 +266,48 @@
             device_id_type=MESH,
         ).start()
 
+    def know_slab():
+        pl.semaphore_wait(row_sem, len(beside))
+        greet_moves(column_sem, column)
+        pl.semaphore_wait(column_sem, len(column))
+        greet_moves(slab_sem, column)
+        pl.semaphore_wait(slab_sem, len(column))
+
     def early_sends():
         for n in range(EARLY):
             only(g != n, functools.partial(send_grp, n))
         send_grp(g)
-        greet_moves(slab_sem, column)
+        greet_moves(row_sem, beside)
+        know_slab()
         pl.semaphore_wait(late_sem, LATE)
+        only(g == EARLY - 1, lambda: greet(near_sem.at[3], EARLY, d))
+        only(g == 0, lambda: greet(near_sem.at[3], GRP - 1, d))
         for n in range(LATE):
             send_grp(EARLY + n)
 
     def late_sends():
         for n in range(EARLY):
             send_grp(n)
+        for_late((-1, 1), lambda to: greet(near_sem.at[0], to, d))
         for n in range(EARLY):
             greet(late_sem, n, other)
-        for_late((-2, 2), lambda to: greet(near_sem.at[0], to, d))
-        greet_moves(slab_sem, column)
-        for_late((-2, 2, -1, 1), send_grp)
+        greet_moves(row_sem, beside)
+        for_late((-1, 1), send_grp)
         send_grp(g)
-        pl.semaphore_wait(near_sem.at[0], in_range(2))
-        for_late((-4, 4), lambda to: greet(near_sem.at[1], to, d))
+        pl.semaphore_wait(near_sem.at[0], in_range(1))
+        for_late((-2, 2), lambda to: greet(near_sem.at[1], to, d))
+        for_late((-2, 2), send_grp)
+        pl.semaphore_wait(near_sem.at[1], in_range(2))
+        for_late((-4, 4), lambda to: greet(near_sem.at[2], to, d))
         for_late((-4, 4, -3, 3), send_grp)
-        pl.semaphore_wait(near_sem.at[1], in_range(4))
-        only(g == EARLY + 1, lambda: greet(near_sem.at[2], EARLY, d))
-        only(g == GRP - 2, lambda: greet(near_sem.at[2], GRP - 1, d))
+        pl.semaphore_wait(near_sem.at[2], in_range(4))
         for_late((-8, 8, -7, 7, -6, 6, -5, 5), send_grp)
-        only((g == EARLY) | (g == GRP - 1), lambda: pl.semaphore_wait(near_sem.at[2], 1))
+        only((g == EARLY) | (g == GRP - 1), lambda: pl.semaphore_wait(near_sem.at[3], 1))
         for_late((-9, 9), send_grp)
+        know_slab()
 
     only(late == 0, early_sends)
     only(late == 1, late_sends)
-    pl.semaphore_wait(slab_sem, len(column))
 
     only(g > 0, lambda: greet(chain_sem, g - 1, other))
     only(g < GRP - 1, lambda: greet(chain_sem, g + 1, other))
@@ -453,7 +464,7 @@
             pltpu.VMEM((DEV, 4, TILE), F32),
             pltpu.VMEM((DEV, 4, TILE), F32),
             pltpu.VMEM((8, TILE), F32),
-            dma((5,)), dma, dma((2,)), dma, dma((1 + len(BOUNDS),)), regular, regular((3,)),
+            dma((5,)), dma, dma((2,)), dma, dma((1 + len(BOUNDS),)), regular, regular((4,)), regular, regular,
             regular, regular, dma, dma, dma((2,)), dma,
         ],
         compiler_params=pltpu.CompilerParams(collective_id=0, has_side_effects=True),

time: 28.4 us -> 28.1 us (0.989)
  no operation moved by 1% of the time
where the time goes in v6:
time: 28.1 us; the launch traced here: 28 us
  Pallas kernels  28 us (100%)
    pallas_call x1, Pallas kernels, per_device(): pl.pallas_call(kernel, out_shape=pltpu.VMEM((864, ELEMS), F32), in_specs=...  27.2 us
    pallas_call x1, Pallas kernels, per_device(): pl.pallas_call(interleave, out_shape=jax.ShapeDtypeStruct((864, ELEMS), F...  0.79 us

profile of v6, /device:TPU:1, one launch (start us, length us, event | category | flops | bytes accessed | tf_op | source)
XLA Modules:
  0.0 28.0 jit_solution(6625663577131771861)
XLA Ops:
  0.0 27.2 %project.1.raw_ref = f32[864,128]{1,0:T(8,128)S(1)} custom-call(f32[3,1024]{1,0:T(4,128)} %pos_hbm.1, f32[3,1024]{1,0:T(4,128)} %frc_hbm.1, f32[1,1024]{1,0:T(1,128)} %bitcast.4, s32[1,1024]{1,0:T(1,128)} %bitcast.5, s32[1,1024]{1,0:T(1,128)} %bitcast.6), custom_call_target="tpu_custom_call" | custom-call | tf_op jit(solution)/shard_map/project/pallas_call | solution.py:447
  27.2 0.8 %interleave.1 = f32[864,128]{1,0:T(8,128)} custom-call(f32[864,128]{1,0:T(8,128)S(1)} %project.1.raw_ref), custom_call_target="tpu_custom_call" | custom-call | tf_op jit(solution)/shard_map/interleave/pallas_call | solution.py:479

commit v7 on v6

--- a/solution.py
+++ b/solution.py
@@ -61,9 +61,9 @@
     return high, mid, rest - mid
 
 
-def pack(positions, forces, volumes, target, element):
+def pack(positions, forces, volumes, target, element, rank):
     dev = target % DEV
-    code = (dev % 2) * 64 + (dev // 2) * SLOTS + rank_in_bin(target)
+    code = (dev % 2) * 64 + (dev // 2) * SLOTS + rank
     row_of = iota((TILE, LOCAL), 0)
     mine = (row_of // 8) == target // DEV
     sub = iota((8, LOCAL), 0)
@@ -248,9 +248,12 @@
     for_late((-1, 1), greet_both)
     only(late == 0, greet_grp)
 
-    for load in loads:
+    loads[0].wait()
+    target = bin_ref[...]
+    rank = rank_in_bin(target)
+    for load in loads[1:]:
         load.wait()
-    packed = pack(pos_ref[...], frc_ref[...], vol_ref[...], bin_ref[...], elem_ref[...])
+    packed = pack(pos_ref[...], frc_ref[...], vol_ref[...], target, elem_ref[...], rank)
     send1[...] = packed.reshape(send1.shape)
 
     greeted = EARLY - 1 + late * (1 + 2 * in_range(1))
@@ -286,9 +289,9 @@
             send_grp(EARLY + n)
 
     def late_sends():
+        for_late((-1, 1), lambda to: greet(near_sem.at[0], to, d))
         for n in range(EARLY):
             send_grp(n)
-        for_late((-1, 1), lambda to: greet(near_sem.at[0], to, d))
         for n in range(EARLY):
             greet(late_sem, n, other)
         greet_moves(row_sem, beside)

time: 28.1 us -> 28.1 us (level)
  no operation moved by 1% of the time
where the time goes in v7:
time: 28.1 us; the launch traced here: 28 us
  Pallas kernels  28 us (100%)
    pallas_call x1, Pallas kernels, per_device(): pl.pallas_call(kernel, out_shape=pltpu.VMEM((864, ELEMS), F32), in_specs=...  27.2 us
    pallas_call x1, Pallas kernels, per_device(): pl.pallas_call(interleave, out_shape=jax.ShapeDtypeStruct((864, ELEMS), F...  0.79 us

profile of v7, /device:TPU:1, one launch (start us, length us, event | category | flops | bytes accessed | tf_op | source)
XLA Modules:
  0.0 28.0 jit_solution(661895222971599777)
XLA Ops:
  0.0 27.2 %project.1.raw_ref = f32[864,128]{1,0:T(8,128)S(1)} custom-call(f32[3,1024]{1,0:T(4,128)} %pos_hbm.1, f32[3,1024]{1,0:T(4,128)} %frc_hbm.1, f32[1,1024]{1,0:T(1,128)} %bitcast.4, s32[1,1024]{1,0:T(1,128)} %bitcast.5, s32[1,1024]{1,0:T(1,128)} %bitcast.6), custom_call_target="tpu_custom_call" | custom-call | tf_op jit(solution)/shard_map/project/pallas_call | solution.py:450
  27.2 0.8 %interleave.1 = f32[864,128]{1,0:T(8,128)} custom-call(f32[864,128]{1,0:T(8,128)S(1)} %project.1.raw_ref), custom_call_target="tpu_custom_call" | custom-call | tf_op jit(solution)/shard_map/interleave/pallas_call | solution.py:482
